TPU v7x, 512 devices: a whole 4x8x8 slice. The times are simulated.
512 devices in a mesh: ty: 16 (over x_lo, z), tx: 32 (over y, x_hi, core).
Axes of the slice: x: 4 (x_hi: 2, x_lo: 2; x = x_hi * 2 + x_lo), y: 8, z: 8, core: 2. Of those that a mesh axis runs over, the one named last changes fastest.
Arguments:
- observed: float32 [6, 2048, 8192], P(None, 'ty', 'tx'), may hold values from -6 to 6
- inverse_variance: float32 [6, 2048, 8192], P(None, 'ty', 'tx'), may hold values from 0.5 to 4
- sed: float32 [16, 32, 6], P('ty', 'tx'), may hold values from 0.2 to 2
- morph: float32 [16, 32, 128, 128], P('ty', 'tx'), may hold values from 0.02 to 1
- foot_block: int32 [16, 32], P('ty', 'tx'), may hold values from 0 to 63, as said below
- gamma: float32 [16, 32], P('ty', 'tx'), may hold values from 0.3 to 1.5
- row_kernel: float32 [6, 41], replicated, may hold values from -1 to 1
- col_kernel: float32 [6, 41], replicated, may hold values from -1 to 1
Outputs:
- residual: float32 [6, 2048, 8192], P(None, 'ty', 'tx')
- new_morph: float32 [16, 32, 128, 128], P('ty', 'tx')
- new_sed: float32 [16, 32, 6], P('ty', 'tx')
Inputs may be any that keep to these rules, and one draw needn't show every extreme that they name: A source's footprint lies in its own tile row, at box column foot_block counted over the whole row; in every tile row at most 2 sources lie in one tile of 2 box columns, and some tile holds exactly 2.
All inputs are finite; a program needn't handle non-finite values.
Results may differ from a plain program's by a relative error of at most 0.0003.
Values sent between devices are 32-bit elements; how exact they have to be, the bound alone decides.
A program may use at most 64 MiB of HBM per device.

v0:
```python
import jax
import jax.numpy as jnp
from jax import lax
from jax.sharding import PartitionSpec as P

HIGHEST_PRECISION = lax.Precision.HIGHEST


def with_halo(value, sides, width):
    for axis, dim in sides:
        devices, length = (lax.axis_size(axis), value.shape[dim])
        up = [(i, (i + 1) % devices) for i in range(devices - 1)]
        down = [(j, i) for i, j in up]
        last = lax.slice_in_dim(value, length - width, length, axis=dim)
        leading = lax.slice_in_dim(value, 0, width, axis=dim)
        before = lax.ppermute(last, axis, up)
        after = lax.ppermute(leading, axis, down)
        value = jnp.concatenate([before, value, after], axis=dim)
    return value


def taps_matrix(kernel, length):
    taps_count = kernel.shape[1]
    span = length + taps_count - 1
    offset = (
        jnp.arange(span, dtype=jnp.int32)[:, None] - jnp.arange(length, dtype=jnp.int32)[None, :]
    )
    select = (offset[None] == jnp.arange(taps_count, dtype=jnp.int32)[:, None, None]).astype(
        jnp.float32
    )
    return jnp.einsum("bt,tqc->bqc", kernel, select, precision=HIGHEST_PRECISION)


def apply_columns(padded, matrix, per_tile, box_size):
    window = matrix.shape[1]
    windows = jnp.stack(
        [padded[:, :, block * box_size : block * box_size + window] for block in range(per_tile)],
        axis=2,
    )
    mixed = jnp.einsum("brjq,bqc->brjc", windows, matrix, precision=HIGHEST_PRECISION)
    return mixed.reshape(padded.shape[0], padded.shape[1], per_tile * box_size)


def body(observed, inverse_variance, sed, morph, foot_block, gamma, row_kernel, col_kernel):
    band_count, tile_rows, tile_cols = observed.shape
    box_size = morph.shape[2]
    per_tile = tile_cols // box_size
    rim_width = (row_kernel.shape[1] - 1) // 2
    all_sed, all_morph, all_foot = (
        lax.all_gather(sed, "tx", axis=1, tiled=True),
        lax.all_gather(morph, "tx", axis=1, tiled=True),
        lax.all_gather(foot_block, "tx", axis=1, tiled=True),
    )
    all_sed = all_sed[0]
    all_morph = all_morph[0]
    all_foot = all_foot[0]
    tile_index = lax.axis_index("tx")
    first_block = tile_index * per_tile
    placed = (
        all_foot[:, None] == first_block + jnp.arange(per_tile, dtype=jnp.int32)[None, :]
    ).astype(jnp.float32)
    weighted = placed[:, None, :] * all_sed[:, :, None]
    model = jnp.einsum("kbj,krc->brjc", weighted, all_morph, precision=HIGHEST_PRECISION).reshape(
        band_count, tile_rows, tile_cols
    )
    flip_rows = taps_matrix(row_kernel[:, ::-1], tile_rows)
    flip_cols = taps_matrix(col_kernel[:, ::-1], box_size)
    wide_model = with_halo(model, (("tx", 2),), rim_width)
    blurred = apply_columns(wide_model, flip_cols, per_tile, box_size)
    tall_blurred = with_halo(blurred, (("ty", 1),), rim_width)
    predicted = jnp.einsum("bqw,bqr->brw", tall_blurred, flip_rows, precision=HIGHEST_PRECISION)
    residual = inverse_variance * (observed - predicted)
    corr_rows = taps_matrix(row_kernel, tile_rows)
    corr_cols = taps_matrix(col_kernel, box_size)
    tall_resid = with_halo(residual, (("ty", 1),), rim_width)
    backrows = jnp.einsum("bqw,bqr->brw", tall_resid, corr_rows, precision=HIGHEST_PRECISION)
    wide_back = with_halo(backrows, (("tx", 2),), rim_width)
    gradient = apply_columns(wide_back, corr_cols, per_tile, box_size)
    grid = gradient.reshape(band_count, tile_rows, per_tile, box_size)
    morph_terms = jnp.einsum("kbj,brjc->krc", weighted, grid, precision=HIGHEST_PRECISION)
    raw_terms = jnp.einsum("krc,brjc->kbj", all_morph, grid, precision=HIGHEST_PRECISION)
    sed_terms = jnp.sum(raw_terms * placed[:, None, :], axis=2)
    morph_grad, sed_grad = (
        lax.psum_scatter(morph_terms, "tx", scatter_dimension=0, tiled=True),
        lax.psum_scatter(sed_terms, "tx", scatter_dimension=0, tiled=True),
    )
    own_sed = sed[0]
    own_morph = morph[0]
    own_gamma = gamma[0]
    step_morph = own_gamma / jnp.sum(own_sed * own_sed, axis=1)
    new_morph = jnp.maximum(own_morph + step_morph[:, None, None] * morph_grad, 0.0)
    step_sed = own_gamma / jnp.sqrt(jnp.sum(own_morph * own_morph, axis=(1, 2)))
    new_sed = jnp.maximum(own_sed + step_sed[:, None] * sed_grad, 0.0)
    return (residual, new_morph[None], new_sed[None])


def solution(mesh):
    in_specs = (
        P(None, "ty", "tx"),
        P(None, "ty", "tx"),
        P("ty", "tx", None),
        P("ty", "tx", None, None),
        P("ty", "tx"),
        P("ty", "tx"),
        P(),
        P(),
    )
    out_specs = (P(None, "ty", "tx"), P("ty", "tx", None, None), P("ty", "tx", None))
    return jax.shard_map(body, mesh=mesh, in_specs=in_specs, out_specs=out_specs, check_vma=False)
```

profile of v0, /device:TPU:96, one launch (start us, length us, event | category | flops | bytes accessed | tf_op | source)
XLA Modules:
  0.0 315.2 jit_solution(1384068626255635407)
XLA Ops:
  9.4 39.6 %all_gather.10 = f32[1,32,6]{2,0,1:T(1,128)S(1)} all-gather(f32[1,1,6]{2,0,1:T(1,128)} %bitcast.108), channel_id=1, replica_groups=mesh['ty'=16,'tx'=32] {'tx'}, dimensions={1}, use_global_device_ids=true | all-gather | bytes 792 | tf_op jit(solution)/shard_map/all_gather | solution.py:50
  51.1 13.8 %all-reduce = s32[32]{0:T(128)S(1)} all-reduce(s32[32]{0:T(128)S(1)} %bitcast_dynamic-update-slice_fusion), channel_id=1, replica_groups=mesh['ty'=16,'tx'=32] {'tx'}, use_global_device_ids=true, to_apply=%add | all-reduce | flops 32 | bytes 256
  65.0 32.4 %all-gather.2.cloned.1.call-done = f32[1,32,128,128]{3,2,0,1:T(8,128)} async-done(((f32[1,1,128,128]{3,2,0,1:T(8,128)}), f32[1,32,128,128]{3,2,0,1:T(8,128)}) %all-gather.2.cloned.1.call-update) | async-done | bytes 2097168 | tf_op jit(solution)/shard_map/all_gather | solution.py:51
  97.4 4.0 %fusion.16 = f32[6,128,2,128]{3,0,1,2:T(8,128)S(1)} fusion(f32[1,32,128,128]{3,2,0,1:T(8,128)} %all-gather.2.cloned.1.call-done, f32[32,6]{0,1:T(8,128)S(1)} %copy.32, f32[32,2]{0,1:T(2,128)S(1)} %compare_convert_fusion), kind=kOutput, calls=%fused_computation.19 | convolution fusion | flops 75497856 | bytes 2884608 | tf_op jit(solution)/shard_map/kbj,krc->brjc/dot_general | solution.py:63
  101.8 2.1 collective-permute-start
  103.9 7.0 %collective-permute-start.1 = (f32[6,128,20]{1,2,0:T(8,128)S(1)}, f32[6,128,20]{1,2,0:T(8,128)S(1)}, u32[]{:S(2)}, u32[]{:S(2)}) collective-permute-start(f32[6,128,20]{1,2,0:T(8,128)S(1)} %get-tuple-element.14), channel_id=1, source_target_pairs={{1,0},{2,1},{3,2},{4,3},{5,4},{6,5},{7,6},{8,7},{9,8},{10,9},{11,1... | collective-permute-start | bytes 184328 | tf_op jit(solution)/shard_map/ppermute | solution.py:17
  114.9 3.7 %collective-permute-start.2 = (f32[6,20,256]{2,1,0:T(8,128)S(1)}, f32[6,20,256]{2,1,0:T(8,128)S(1)}, u32[]{:S(2)}, u32[]{:S(2)}) collective-permute-start(f32[6,20,256]{2,1,0:T(8,128)S(1)} %get-tuple-element.9), channel_id=1, source_target_pairs={{0,32},{32,64},{64,96},{96,128},{128,160},{160,192},{192,224},{224... | collective-permute-start | bytes 368648 | tf_op jit(solution)/shard_map/ppermute | solution.py:16
  118.6 2.3 collective-permute-start.3
  122.4 3.2 %collective-permute-done.3 = f32[6,20,256]{2,1,0:T(8,128)S(1)} collective-permute-done((f32[6,20,256]{2,1,0:T(8,128)S(1)}, f32[6,20,256]{2,1,0:T(8,128)S(1)}, u32[]{:S(2)}, u32[]{:S(2)}) %collective-permute-start.3) | collective-permute-done | bytes 122912 | tf_op jit(solution)/shard_map/ppermute | solution.py:17
  125.6 1.5 fusion.19
  127.2 4.4 %collective-permute-start.4 = (f32[6,20,256]{2,1,0:T(8,128)S(1)}, f32[6,20,256]{2,1,0:T(8,128)S(1)}, u32[]{:S(2)}, u32[]{:S(2)}) collective-permute-start(f32[6,20,256]{2,1,0:T(8,128)S(1)} %get-tuple-element.7), channel_id=1, source_target_pairs={{0,32},{32,64},{64,96},{96,128},{128,160},{160,192},{192,224},{224... | collective-permute-start | bytes 368648 | tf_op jit(solution)/shard_map/ppermute | solution.py:16
  131.6 2.1 collective-permute-start.5
  135.2 4.6 %collective-permute-done.5 = f32[6,20,256]{2,1,0:T(8,128)S(1)} collective-permute-done((f32[6,20,256]{2,1,0:T(8,128)S(1)}, f32[6,20,256]{2,1,0:T(8,128)S(1)}, u32[]{:S(2)}, u32[]{:S(2)}) %collective-permute-start.5) | collective-permute-done | bytes 122912 | tf_op jit(solution)/shard_map/ppermute | solution.py:17
  139.9 1.5 fusion.44
  141.6 1.9 collective-permute-start.6
  143.5 7.3 %collective-permute-start.7 = (f32[6,128,20]{2,1,0:T(8,128)S(1)}, f32[6,128,20]{2,1,0:T(8,128)S(1)}, u32[]{:S(2)}, u32[]{:S(2)}) collective-permute-start(f32[6,128,20]{2,1,0:T(8,128)S(1)} %get-tuple-element.6), channel_id=1, source_target_pairs={{1,0},{2,1},{3,2},{4,3},{5,4},{6,5},{7,6},{8,7},{9,8},{10,9},{11,1... | collective-permute-start | bytes 184328 | tf_op jit(solution)/shard_map/ppermute | solution.py:17
  152.3 2.1 collective-permute-done.6
  154.4 1.7 collective-permute-done.7
  156.6 1.6 fusion.14
  158.2 2.5 convolution_bitcast_fusion
  160.7 2.5 copy.45
  165.4 4.6 %fusion.30 = f32[32,6]{0,1:T(8,128)S(1)} fusion(f32[1,32,128,128]{3,2,0,1:T(8,128)S(1)} %copy-done, f32[6,128,2,128]{3,1,2,0:T(8,128)S(1)} %fusion.14, f32[32,2]{0,1:T(2,128)S(1)} %compare_convert_fusion), kind=kOutput, calls=%fused_computation.28 | convolution fusion | flops 75498048 | bytes 2884608 | tf_op jit(solution)/shard_map/krc,brjc->kbj/dot_general | solution.py:81
  170.2 134.2 %all-reduce.1 = f32[32,6]{1,0:T(8,128)S(1)} all-reduce(f32[32,6]{1,0:T(8,128)S(1)} %copy.47), channel_id=3, replica_groups=mesh['ty'=16,'tx'=32] {'tx'}, use_global_device_ids=true, to_apply=%region_4.0.clone | all-reduce | flops 192 | bytes 1536
  304.4 2.1 fusion.60
  (50 shorter events, 15.2 us)
Async XLA Ops:
  7.2 90.2 %all-gather.2.cloned.1.call-start = ((), (), s32[]{:S(2)}) async-start(), calls=%async_computation.1 | async-start | bytes 2162688 | tf_op jit(solution)/shard_map/all_gather | solution.py:51
  7.9 296.5 %reduce-scatter.2.cloned.1.call-start = ((), (), s32[]{:S(2)}) async-start(), calls=%async_computation.2 | async-start | bytes 2162688 | tf_op jit(solution)/shard_map/reduce_scatter | solution.py:84
  101.4 11.0 %copy-start.5 = (f32[6,41]{1,0:T(8,128)S(1)}, f32[6,41]{1,0:T(8,128)}, u32[]{:S(2)}) copy-start(f32[6,41]{1,0:T(8,128)} %param.14) | copy-start | bytes 2956
  101.8 10.8 %collective-permute-start = (f32[6,128,20]{1,2,0:T(8,128)S(1)}, f32[6,128,20]{1,2,0:T(8,128)S(1)}, u32[]{:S(2)}, u32[]{:S(2)}) collective-permute-start(f32[6,128,20]{1,2,0:T(8,128)S(1)} %get-tuple-element.13), channel_id=1, source_target_pairs={{0,1},{1,2},{2,3},{3,4},{4,5},{5,6},{6,7},{7,8},{8,9},{9,10},{10,1... | collective-permute-start | bytes 184328 | tf_op jit(solution)/shard_map/ppermute | solution.py:16
  103.9 9.0 %collective-permute-start.1 = (f32[6,128,20]{1,2,0:T(8,128)S(1)}, f32[6,128,20]{1,2,0:T(8,128)S(1)}, u32[]{:S(2)}, u32[]{:S(2)}) collective-permute-start(f32[6,128,20]{1,2,0:T(8,128)S(1)} %get-tuple-element.14), channel_id=1, source_target_pairs={{1,0},{2,1},{3,2},{4,3},{5,4},{6,5},{7,6},{8,7},{9,8},{10,9},{11,1... | collective-permute-start | bytes 184328 | tf_op jit(solution)/shard_map/ppermute | solution.py:17
  114.5 11.1 %copy-start.2 = (f32[6,128,256]{2,1,0:T(8,128)S(1)}, f32[6,128,256]{2,1,0:T(8,128)}, u32[]{:S(2)}) copy-start(f32[6,128,256]{2,1,0:T(8,128)} %param.9) | copy-start | bytes 2359300
  114.6 11.1 %copy-start.3 = (f32[6,128,256]{2,1,0:T(8,128)S(1)}, f32[6,128,256]{2,1,0:T(8,128)}, u32[]{:S(2)}) copy-start(f32[6,128,256]{2,1,0:T(8,128)} %param.8) | copy-start | bytes 2359300
  114.9 7.5 %collective-permute-start.2 = (f32[6,20,256]{2,1,0:T(8,128)S(1)}, f32[6,20,256]{2,1,0:T(8,128)S(1)}, u32[]{:S(2)}, u32[]{:S(2)}) collective-permute-start(f32[6,20,256]{2,1,0:T(8,128)S(1)} %get-tuple-element.9), channel_id=1, source_target_pairs={{0,32},{32,64},{64,96},{96,128},{128,160},{160,192},{192,224},{224... | collective-permute-start | bytes 368648 | tf_op jit(solution)/shard_map/ppermute | solution.py:16
  118.6 7.0 %collective-permute-start.3 = (f32[6,20,256]{2,1,0:T(8,128)S(1)}, f32[6,20,256]{2,1,0:T(8,128)S(1)}, u32[]{:S(2)}, u32[]{:S(2)}) collective-permute-start(f32[6,20,256]{2,1,0:T(8,128)S(1)} %get-tuple-element.10), channel_id=1, source_target_pairs={{32,0},{64,32},{96,64},{128,96},{160,128},{192,160},{224,192},{256... | collective-permute-start | bytes 368648 | tf_op jit(solution)/shard_map/ppermute | solution.py:17
  127.2 14.4 %copy-start.1 = (f32[6,128,256]{2,1,0:T(8,128)}, f32[6,128,256]{2,1,0:T(8,128)S(1)}, u32[]{:S(2)}) copy-start(f32[6,128,256]{2,1,0:T(8,128)S(1)} %fusion.19) | copy-start | bytes 2359300
  127.2 8.0 %collective-permute-start.4 = (f32[6,20,256]{2,1,0:T(8,128)S(1)}, f32[6,20,256]{2,1,0:T(8,128)S(1)}, u32[]{:S(2)}, u32[]{:S(2)}) collective-permute-start(f32[6,20,256]{2,1,0:T(8,128)S(1)} %get-tuple-element.7), channel_id=1, source_target_pairs={{0,32},{32,64},{64,96},{96,128},{128,160},{160,192},{192,224},{224... | collective-permute-start | bytes 368648 | tf_op jit(solution)/shard_map/ppermute | solution.py:16
  131.6 8.2 %collective-permute-start.5 = (f32[6,20,256]{2,1,0:T(8,128)S(1)}, f32[6,20,256]{2,1,0:T(8,128)S(1)}, u32[]{:S(2)}, u32[]{:S(2)}) collective-permute-start(f32[6,20,256]{2,1,0:T(8,128)S(1)} %get-tuple-element.8), channel_id=1, source_target_pairs={{32,0},{64,32},{96,64},{128,96},{160,128},{192,160},{224,192},{256... | collective-permute-start | bytes 368648 | tf_op jit(solution)/shard_map/ppermute | solution.py:17
  135.2 15.6 %copy-start.6 = (f32[6,41]{1,0:T(8,128)S(1)}, f32[6,41]{1,0:T(8,128)}, u32[]{:S(2)}) copy-start(f32[6,41]{1,0:T(8,128)} %param.15) | copy-start | bytes 2956
  141.6 12.8 %collective-permute-start.6 = (f32[6,128,20]{2,1,0:T(8,128)S(1)}, f32[6,128,20]{2,1,0:T(8,128)S(1)}, u32[]{:S(2)}, u32[]{:S(2)}) collective-permute-start(f32[6,128,20]{2,1,0:T(8,128)S(1)} %get-tuple-element.5), channel_id=1, source_target_pairs={{0,1},{1,2},{2,3},{3,4},{4,5},{5,6},{6,7},{7,8},{8,9},{9,10},{10,1... | collective-permute-start | bytes 184328 | tf_op jit(solution)/shard_map/ppermute | solution.py:16
  143.5 12.5 %collective-permute-start.7 = (f32[6,128,20]{2,1,0:T(8,128)S(1)}, f32[6,128,20]{2,1,0:T(8,128)S(1)}, u32[]{:S(2)}, u32[]{:S(2)}) collective-permute-start(f32[6,128,20]{2,1,0:T(8,128)S(1)} %get-tuple-element.6), channel_id=1, source_target_pairs={{1,0},{2,1},{3,2},{4,3},{5,4},{6,5},{7,6},{8,7},{9,8},{10,9},{11,1... | collective-permute-start | bytes 184328 | tf_op jit(solution)/shard_map/ppermute | solution.py:17
  163.3 0.8 copy-start.7
  163.3 2.1 copy-start
  163.3 141.1 %copy-start.4 = (f32[1,1,128,128]{3,2,1,0:T(8,128)S(1)}, f32[1,1,128,128]{3,2,1,0:T(8,128)}, u32[]{:S(2)}) copy-start(f32[1,1,128,128]{3,2,1,0:T(8,128)} %param.11) | copy-start | bytes 196612
Sparse Core Ops, SparseCore 0:
  11.3 86.0 all-gather.1
  163.4 126.2 reduce-scatter.1
where the time goes:
time: 316 us; the launch traced here: 315 us
  blocking collectives  188 us (59%)
  waiting for transfers between devices  45.2 us (14%)
  starting transfers between devices  30.9 us (10%)
  matrix products  23.3 us (7%)
  between operations  17.1 us (5%)
  local copies, waits for them, and re-layouts  6.49 us (2%)
  other arithmetic  4.64 us (1%)
    unnamed x2, blocking collectives  148 us
    all_gather x1, blocking collectives, body(): lax.all_gather(sed, 'tx', axis=1, tiled=True)  39.6 us
    all_gather x1, waiting for transfers between devices, body(): lax.all_gather(morph, 'tx', axis=1, tiled=True)  32.4 us
    ppermute x4, starting transfers between devices, with_halo(): after = lax.ppermute(leading, axis, down)  18.7 us
    ppermute x4, starting transfers between devices, with_halo(): before = lax.ppermute(last, axis, up)  12.1 us
    ppermute x4, waiting for transfers between devices, with_halo(): after = lax.ppermute(leading, axis, down)  9.93 us
  transfers between devices with their start and end apart: 10, of which 6 were waited for; matrix products, arithmetic and copies ran while one was open for 5% of the time, Pallas kernels for 0%

commit v1 on v0

v1 whole, which is shorter than its diff:
```python
import functools

import jax
import jax.numpy as jnp
from jax import lax
from jax.experimental import pallas as pl
from jax.experimental.pallas import tpu as pltpu
from jax.sharding import PartitionSpec as P

MESH = pl.DeviceIdType.MESH
F32 = jnp.float32
BF16 = jnp.bfloat16
HIGHEST = lax.Precision.HIGHEST
BOX = 128
HALO = 24
WIDE = 384
NAR = 256


def up8(n):
    return (n + 7) // 8 * 8


def iota(shape, dim):
    return lax.broadcasted_iota(jnp.int32, shape, dim)


def split(x):
    hi = x.astype(BF16)
    return hi, (x - hi.astype(F32)).astype(BF16)


def dot(a, b):
    return jnp.dot(a, b, preferred_element_type=F32)


def exact(a, b):
    return jnp.dot(a, b, preferred_element_type=F32, precision=HIGHEST)


def kernel(
    nty, ntx, bands, taps,
    obs_hbm, iv_hbm, sed_s, morph_hbm, foot_s, gamma_s, rk_hbm, ck_hbm,
    resid_hbm, nmorph_ref, nsed_ref,
    obs_e, iv_e, res_e, model_e, west1, east1, west2, east2, sw1, se1, sw2, se2,
    morph_v, ob1, ib1, ob2, ib2, ob3, ib3, ob4, ib4, sg_send, sg_in,
    slots, sinfo, nslots, sslots, ninfo, soinfo, grads, sgacc,
    wtab, mtab, rk_v, ck_v, ktab_c, ktab_r, tcol, trow1, trow2, ext_h, ext_l,
    loc_sem, send_sem, a2a_sem, obs_sem, sl_sem, st_sem,
):
    ti = lax.axis_index("ty")
    me = lax.axis_index("tx")
    reach = (taps - 1) // 2
    rows = BOX // ntx
    m1, m2, m4 = up8(rows + 1), 2 * rows, up8(rows)
    deep = 2 * HALO
    ext1, ext2 = BOX + 2 * deep, BOX + 2 * HALO
    north, south = lax.rem(ti + nty - 1, nty), lax.rem(ti + 1, nty)
    west, east = lax.rem(me + ntx - 1, ntx), lax.rem(me + 1, ntx)

    barrier = pltpu.get_barrier_semaphore()

    def greet(j, carry):
        pl.semaphore_signal(
            barrier, inc=1, device_id=(ti, lax.rem(me + j, ntx)), device_id_type=MESH
        )
        return carry

    lax.fori_loop(1, ntx, greet, 0)
    for yy in (north, south):
        for xx in (me, west, east):
            pl.semaphore_signal(barrier, inc=1, device_id=(yy, xx), device_id_type=MESH)

    load_morph = pltpu.make_async_copy(morph_hbm.at[0, 0], morph_v, loc_sem.at[0])
    load_rk = pltpu.make_async_copy(rk_hbm, rk_v, loc_sem.at[1])
    load_ck = pltpu.make_async_copy(ck_hbm, ck_v, loc_sem.at[2])
    load_obs = pltpu.make_async_copy(obs_hbm, obs_e.at[:, HALO : HALO + BOX, :], loc_sem.at[3])
    load_iv = pltpu.make_async_copy(iv_hbm, iv_e.at[:, HALO : HALO + BOX, :], loc_sem.at[4])
    load_morph.start()
    load_rk.start()
    load_ck.start()
    load_obs.start()
    load_iv.start()

    foot = foot_s[0, 0]
    tile = foot // 2
    box = foot - 2 * tile
    lane1 = iota((1, BOX), 1)
    info = jnp.zeros((1, BOX), F32)
    for b in range(bands):
        info = jnp.where(lane1 == b, sed_s[0, 0, b], info)
    info = jnp.where(lane1 == 6, tile.astype(F32), info)
    info = jnp.where(lane1 == 7, box.astype(F32), info)
    ob1[...] = jnp.zeros_like(ob1)
    ob4[...] = jnp.zeros_like(ob4)
    ob1[pl.ds(rows, ntx, stride=m1), :] = jnp.broadcast_to(info, (ntx, BOX))
    load_morph.wait()
    for r in range(rows):
        ob1[pl.ds(r, ntx, stride=m1), :] = morph_v[pl.ds(r, ntx, stride=rows), :]

    def exchange(out, arrived, m, phase):
        def step(j, carry):
            p = lax.rem(me + j, ntx)
            pltpu.make_async_remote_copy(
                out.at[pl.ds(pl.multiple_of(p * m, 8), m)],
                arrived.at[pl.ds(pl.multiple_of(me * m, 8), m)],
                send_sem.at[phase], a2a_sem.at[phase],
                device_id=(ti, p), device_id_type=MESH,
            ).start()
            return carry

        lax.fori_loop(1, ntx, step, 0)
        mine = pl.ds(pl.multiple_of(me * m, 8), m)
        arrived[mine, :] = out[mine, :]

    def whole(out, arrived, m, phase):
        part = pl.ds(0, (ntx - 1) * m)
        return pltpu.make_async_remote_copy(
            out.at[part], arrived.at[part], send_sem.at[phase], a2a_sem.at[phase],
            device_id=(ti, east), device_id_type=MESH,
        )

    pl.semaphore_wait(barrier, ntx - 1 + 6)
    exchange(ob1, ib1, m1, 0)

    def send(src, dst, s_sem, r_sem, yy, xx):
        copy = pltpu.make_async_remote_copy(
            src, dst, s_sem, r_sem, device_id=(yy, xx), device_id_type=MESH
        )
        copy.start()
        return copy

    low, high = slice(0, HALO), slice(BOX - HALO, BOX)
    far = slice(HALO + BOX, ext2)
    images = []
    for n, (src, dst) in enumerate(((obs_hbm, obs_e), (iv_hbm, iv_e))):
        images.append(send(src.at[:, high, :], dst.at[:, low, :], obs_sem.at[0, 2 * n], obs_sem.at[1, 2 * n], south, me))
        images.append(send(src.at[:, low, :], dst.at[:, far, :], obs_sem.at[0, 2 * n + 1], obs_sem.at[1, 2 * n + 1], north, me))

    load_rk.wait()
    load_ck.wait()
    flip = (iota((BOX, BOX), 0) + iota((BOX, BOX), 1) == taps - 1).astype(F32)

    for table, values, forward in ((ktab_c, ck_v, 0), (ktab_r, rk_v, 1)):
        table[...] = jnp.zeros_like(table)
        table[forward, 0, 0:bands, 0:taps] = values[...]
        plain = table[forward, 0, :, 0:BOX]
        table[1 - forward, 0, :, 0:BOX] = exact(plain, flip)
        for st in range(2):
            full = table[st, 0, :, 0:BOX]
            hi = full.astype(BF16).astype(F32)
            table[st, 0, :, 0:BOX] = hi
            table[st, 1, :, 0:BOX] = full - hi

    def band_tables(st, b):
        strip_row = iota((BOX, NAR), 0)
        inside = (strip_row >= reach * b) & (strip_row < reach * b + reach)
        for part in range(2):
            spread = jnp.broadcast_to(ktab_c[st, part, pl.ds(b, 1), :], (BOX, WIDE))
            skew = pltpu.roll(spread, 0, 1, stride=1, stride_axis=0)
            for n in range(2):
                own = pltpu.roll(skew, (WIDE - reach + n * BOX) % WIDE, 1)[:, 0:NAR]
                tcol[st, b, part, n * BOX : (n + 1) * BOX, :] = own.astype(BF16)
            for n, shift in enumerate((WIDE - 2 * reach, NAR - reach)):
                side = pltpu.roll(skew, shift - reach * b, 1)[:, 0:NAR]
                side = jnp.where(inside, side, 0.0).astype(BF16)
                tcol[st, b, part, NAR + n * BOX : NAR + (n + 1) * BOX, :] = side
            spread = jnp.broadcast_to(ktab_r[st, part, pl.ds(b, 1), :], (BOX, NAR))
            skew = pltpu.roll(spread, 0, 1, stride=1, stride_axis=0)
            out, trow = ((ext2, trow1), (BOX, trow2))[st]
            for n in range(0, out, BOX):
                count = min(BOX, out - n)
                own = pltpu.roll(skew, (HALO - reach + n) % NAR, 1)
                trow[b, part, n : n + count] = own[0:count, 0 : trow.shape[3]].astype(BF16)

    for b in range(bands):
        band_tables(0, b)

    whole(ob1, ib1, m1, 0).wait_recv()
    infos = ib1[pl.ds(rows, ntx, stride=m1), :]
    wide = (ntx, BOX)
    row_i, lane_i = iota(wide, 0), iota(wide, 1)
    tile_col = jnp.broadcast_to(infos[:, 6:7], wide)
    tile_row = jnp.sum(jnp.where(row_i == lane_i, tile_col, 0.0), axis=0, keepdims=True)
    tile_row = jnp.broadcast_to(jnp.where(lane1 < ntx, tile_row, -1.0), wide)
    same = tile_col == tile_row
    slot_row = jnp.sum(jnp.where(same & (row_i < lane_i), 1.0, 0.0), axis=0, keepdims=True)
    slot_row = jnp.broadcast_to(slot_row, wide)
    slot_col = jnp.sum(jnp.where(same & (lane_i < row_i), 1.0, 0.0), axis=1, keepdims=True)
    slot_col = jnp.broadcast_to(slot_col, wide)
    target = row_i.astype(F32)
    pick = [
        jnp.where((tile_row == target) & (slot_row == float(s)), 1.0, 0.0)[:, 0:ntx]
        for s in range(2)
    ]
    pieces = jnp.concatenate([ib1[pl.ds(r, ntx, stride=m1), :] for r in range(rows)], axis=1)
    chosen = exact(jnp.concatenate(pick, axis=0), pieces)
    for s in range(2):
        for r in range(rows):
            ob2[pl.ds(s * rows + r, ntx, stride=m2), :] = chosen[
                s * ntx : (s + 1) * ntx, r * BOX : (r + 1) * BOX
            ]
    exchange(ob2, ib2, m2, 1)

    here = me.astype(F32)
    for s in range(2):
        mine = (tile_col == here) & (slot_col == float(s))
        sinfo[pl.ds(s, 1), :] = jnp.sum(jnp.where(mine, infos, 0.0), axis=0, keepdims=True)
    sinfo[2:8, :] = jnp.zeros((6, BOX), F32)
    lane_f = lane_i.astype(F32)
    give = jnp.concatenate(
        [
            jnp.where((tile_col == lane_f) & (slot_col == float(s)), 1.0, 0.0)[:, 0:ntx]
            for s in range(2)
        ],
        axis=1,
    )
    own_tile = tile.astype(F32)
    own_slot = jnp.sum(
        jnp.where(row_i[:, 0:1] == me, slot_col[:, 0:1], 0.0), axis=0, keepdims=True
    )

    eye8 = iota((8, BOX), 0) == iota((8, BOX), 1)

    def tables(which, ref, live):
        for s in range(2):
            line = jnp.broadcast_to(ref[pl.ds(s, 1), :], (8, BOX))
            column = jnp.sum(jnp.where(eye8, line, 0.0), axis=1, keepdims=True)
            table = jnp.broadcast_to(column, (8, BOX)) * live
            boxes = jnp.broadcast_to(column[7:8], (8, BOX))
            for j in range(2):
                wtab[which, s, j] = jnp.where(boxes == float(j), table, 0.0)
                if which == 1:
                    mtab[s, j] = jnp.where(boxes == float(j), 1.0, 0.0)

    tables(1, sinfo, 1.0)
    for b in range(bands):
        band_tables(1, b)

    whole(ob2, ib2, m2, 1).wait_recv()
    for s in range(2):
        for r in range(rows):
            slots[s, pl.ds(r, ntx, stride=rows), :] = ib2[pl.ds(s * rows + r, ntx, stride=m2), :]

    waits = []
    for n, (src, dst, yy) in enumerate(
        (
            (slots.at[:, BOX - deep : BOX, :], nslots, south),
            (slots.at[:, 0:deep, :], sslots, north),
            (sinfo, ninfo, south),
            (sinfo, soinfo, north),
        )
    ):
        waits.append(send(src, dst, sl_sem.at[0, n], sl_sem.at[1, n], yy, me))

    sw1[...] = jnp.zeros_like(sw1)
    se1[...] = jnp.zeros_like(se1)
    tile_lane = iota((BOX, BOX), 1)
    for b in range(bands):
        for j in range(2):
            part = sum(wtab[1, s, j, pl.ds(b, 1), :] * slots[s] for s in range(2))
            model_e[b, deep : deep + BOX, j * BOX : (j + 1) * BOX] = part
            keep = (tile_lane >= reach * b) & (tile_lane < reach * b + reach)
            shift = (reach * b) if j == 0 else (reach * b + reach) % BOX
            moved = pltpu.roll(part, shift, 1) if shift else part
            ref = (sw1, se1)[j]
            ref[...] = jnp.where(keep, moved, ref[...])
    for n, (src, dst, yy, xx) in enumerate(
        (
            (se1, west1.at[deep : deep + BOX], ti, east),
            (sw1, east1.at[deep : deep + BOX], ti, west),
            (se1.at[BOX - deep : BOX], west1.at[0:deep], south, east),
            (sw1.at[BOX - deep : BOX], east1.at[0:deep], south, west),
            (se1.at[0:deep], west1.at[deep + BOX : ext1], north, east),
            (sw1.at[0:deep], east1.at[deep + BOX : ext1], north, west),
        )
    ):
        waits.append(send(src, dst, sl_sem.at[0, 4 + n], sl_sem.at[1, 4 + n], yy, xx))

    for copy in waits[0:4]:
        copy.wait_recv()
    tables(0, ninfo, jnp.where(ti > 0, 1.0, 0.0))
    tables(2, soinfo, jnp.where(ti < nty - 1, 1.0, 0.0))

    for b in range(bands):
        for which, ref, start in ((0, nslots, 0), (2, sslots, deep + BOX)):
            for j in range(2):
                part = sum(wtab[which, s, j, pl.ds(b, 1), :] * ref[s] for s in range(2))
                model_e[b, start : start + deep, j * BOX : (j + 1) * BOX] = part

    load_obs.wait()
    load_iv.wait()
    for copy in images:
        copy.wait_recv()
    for copy in waits[4:]:
        copy.wait_recv()

    def halo_parts(left, right, count, edge):
        row = iota((count, BOX), 0)
        inner = ((row >= edge) | (ti > 0)) & ((row < count - edge) | (ti < nty - 1))
        for n, (ref, ok) in enumerate(((left, me > 0), (right, me < ntx - 1))):
            hi, lo = split(jnp.where(inner & ok, ref[...], 0.0))
            ext_h[0:count, n * BOX : (n + 1) * BOX] = hi
            ext_l[0:count, n * BOX : (n + 1) * BOX] = lo

    def passes(st, b, image, count, trow):
        hi, lo = split(image)
        hi = jnp.concatenate([hi, ext_h[0:count, :]], axis=1)
        lo = jnp.concatenate([lo, ext_l[0:count, :]], axis=1)
        mixed = dot(hi, tcol[st, b, 0]) + (dot(hi, tcol[st, b, 1]) + dot(lo, tcol[st, b, 0]))
        hi, lo = split(mixed)
        return dot(trow[b, 0], hi) + (dot(trow[b, 0], lo) + dot(trow[b, 1], hi))

    halo_parts(west1, east1, ext1, deep)
    sw2[...] = jnp.zeros_like(sw2)
    se2[...] = jnp.zeros_like(se2)
    row = iota((ext2, 2 * BOX), 0)
    inside = ((row >= HALO) | (ti > 0)) & ((row < HALO + BOX) | (ti < nty - 1))
    lane = iota((ext2, BOX), 1)

    def first(b, carry):
        predicted = passes(0, b, model_e[b], ext1, trow1)
        residual = jnp.where(inside, iv_e[b] * (obs_e[b] - predicted), 0.0)
        res_e[b] = residual
        keep = (lane >= reach * b) & (lane < reach * b + reach)
        moved = pltpu.roll(residual[:, 0:BOX], reach * b, 1)
        sw2[...] = jnp.where(keep, moved, sw2[...])
        moved = pltpu.roll(residual[:, BOX:], lax.rem(reach * b + reach, BOX), 1)
        se2[...] = jnp.where(keep, moved, se2[...])
        return carry

    lax.fori_loop(0, bands, first, 0)
    strips = [
        send(se2, west2, st_sem.at[0, 0], st_sem.at[1, 0], ti, east),
        send(sw2, east2, st_sem.at[0, 1], st_sem.at[1, 1], ti, west),
    ]
    store = pltpu.make_async_copy(res_e.at[:, HALO : HALO + BOX, :], resid_hbm, loc_sem.at[5])
    store.start()
    grads[...] = jnp.zeros_like(grads)
    sgacc[...] = jnp.zeros_like(sgacc)
    for copy in strips:
        copy.wait_recv()
    halo_parts(west2, east2, ext2, HALO)

    def second(b, carry):
        gradient = passes(1, b, res_e[b], ext2, trow2)
        halves = (gradient[:, 0:BOX], gradient[:, BOX:])
        for s in range(2):
            grads[s] += sum(wtab[1, s, j, pl.ds(b, 1), :] * halves[j] for j in range(2))
            under = sum(mtab[s, j, pl.ds(b, 1), :] * halves[j] for j in range(2))
            sgacc[s, pl.ds(b, 1), :] = jnp.sum(slots[s] * under, axis=0, keepdims=True)
        return carry

    lax.fori_loop(0, bands, second, 0)

    for s in range(2):
        for r in range(rows):
            ob3[pl.ds(s * rows + r, ntx, stride=m2), :] = grads[s, pl.ds(r, ntx, stride=rows), :]
    exchange(ob3, ib3, m2, 2)
    line = jnp.zeros((1, BOX), F32)
    for s in range(2):
        column = jnp.broadcast_to(jnp.sum(sgacc[s], axis=1, keepdims=True), (8, BOX))
        mark = iota((8, BOX), 1) == iota((8, BOX), 0) + 8 * s
        line = line + jnp.sum(jnp.where(mark, column, 0.0), axis=0, keepdims=True)
    sg_send[0] = line
    sg_in[me] = line

    def spread_sed(j, carry):
        p = lax.rem(me + j, ntx)
        pltpu.make_async_remote_copy(
            sg_send.at[0], sg_in.at[me], send_sem.at[4], a2a_sem.at[4],
            device_id=(ti, p), device_id_type=MESH,
        ).start()
        return carry

    lax.fori_loop(1, ntx, spread_sed, 0)

    whole(ob3, ib3, m2, 2).wait_recv()
    pieces = jnp.concatenate(
        [
            jnp.concatenate(
                [ib3[pl.ds(s * rows + r, ntx, stride=m2), :] for r in range(rows)], axis=1
            )
            for s in range(2)
        ],
        axis=0,
    )
    chosen = exact(give, pieces)
    for r in range(rows):
        ob4[pl.ds(r, ntx, stride=m4), :] = chosen[:, r * BOX : (r + 1) * BOX]
    exchange(ob4, ib4, m4, 3)

    square = jnp.sum(jnp.where(lane1 < bands, info * info, 0.0), axis=1, keepdims=True)
    step_morph = gamma_s[0, 0] / square
    full = morph_v[...]
    norm = jnp.sum(jnp.sum(full * full, axis=0, keepdims=True), axis=1, keepdims=True)
    step_sed = gamma_s[0, 0] / jnp.sqrt(norm)

    part = pl.ds(0, ntx - 1)
    seds = pltpu.make_async_remote_copy(
        sg_in.at[part], sg_in.at[part], send_sem.at[4], a2a_sem.at[4],
        device_id=(ti, east), device_id_type=MESH,
    )
    seds.wait_recv()
    terms = jnp.zeros((1, BOX), F32)
    for d in range(ntx):
        terms = terms + jnp.where(own_tile == float(d), sg_in[d], 0.0)
    terms = jnp.where(own_slot == 0.0, terms, pltpu.roll(terms, BOX - 8, 1))
    nsed_ref[0] = jnp.maximum(info + step_sed * terms, 0.0)[:, 0:bands]

    whole(ob4, ib4, m4, 3).wait_recv()
    for r in range(rows):
        at = pl.ds(r, ntx, stride=rows)
        update = step_morph * ib4[pl.ds(r, ntx, stride=m4), :]
        nmorph_ref[0, 0, at, :] = jnp.maximum(morph_v[at, :] + update, 0.0)

    whole(ob1, ib1, m1, 0).wait_send()
    whole(ob2, ib2, m2, 1).wait_send()
    whole(ob3, ib3, m2, 2).wait_send()
    whole(ob4, ib4, m4, 3).wait_send()
    seds.wait_send()
    for copy in images + waits + strips:
        copy.wait_send()
    store.wait()


def solution(mesh):
    nty, ntx = mesh.shape["ty"], mesh.shape["tx"]

    def body(observed, inverse_variance, sed, morph, foot_block, gamma, row_kernel, col_kernel):
        bands, height, width = observed.shape
        taps = row_kernel.shape[1]
        rows = BOX // ntx
        m1, m2, m4 = up8(rows + 1), 2 * rows, up8(rows)
        deep = 2 * HALO
        ext1, ext2 = height + 2 * deep, height + 2 * HALO

        def vmem(*shape, dtype=F32):
            return pltpu.VMEM(shape, dtype)

        scratch = [
            vmem(bands, ext2, width), vmem(bands, ext2, width), vmem(bands, ext2, width),
            vmem(bands, ext1, width),
            vmem(ext1, BOX), vmem(ext1, BOX), vmem(ext2, BOX), vmem(ext2, BOX),
            vmem(BOX, BOX), vmem(BOX, BOX), vmem(ext2, BOX), vmem(ext2, BOX),
            vmem(BOX, BOX),
            vmem(ntx * m1, BOX), vmem(ntx * m1, BOX), vmem(ntx * m2, BOX), vmem(ntx * m2, BOX),
            vmem(ntx * m2, BOX), vmem(ntx * m2, BOX), vmem(ntx * m4, BOX), vmem(ntx * m4, BOX),
            vmem(1, 1, BOX), vmem(ntx, 1, BOX),
            vmem(2, BOX, BOX), vmem(8, BOX), vmem(2, deep, BOX), vmem(2, deep, BOX),
            vmem(8, BOX), vmem(8, BOX), vmem(2, BOX, BOX), vmem(2, 8, BOX),
            vmem(3, 2, 2, 8, BOX), vmem(2, 2, 8, BOX),
            vmem(bands, taps), vmem(bands, taps),
            vmem(2, 2, 8, WIDE), vmem(2, 2, 8, NAR),
            vmem(2, bands, 2, 2 * NAR, NAR, dtype=BF16),
            vmem(bands, 2, ext2, ext1, dtype=BF16), vmem(bands, 2, BOX, ext2, dtype=BF16),
            vmem(ext1, NAR, dtype=BF16), vmem(ext1, NAR, dtype=BF16),
            pltpu.SemaphoreType.DMA((6,)), pltpu.SemaphoreType.DMA((5,)),
            pltpu.SemaphoreType.DMA((5,)), pltpu.SemaphoreType.DMA((2, 4)),
            pltpu.SemaphoreType.DMA((2, 10)), pltpu.SemaphoreType.DMA((2, 2)),
        ]
        anywhere = pl.BlockSpec(memory_space=pl.ANY)
        scalars = pl.BlockSpec(memory_space=pltpu.SMEM)
        vector = pl.BlockSpec(memory_space=pltpu.VMEM)
        return pl.pallas_call(
            functools.partial(kernel, nty, ntx, bands, taps),
            out_shape=(
                jax.ShapeDtypeStruct(observed.shape, F32),
                jax.ShapeDtypeStruct(morph.shape, F32),
                jax.ShapeDtypeStruct(sed.shape, F32),
            ),
            in_specs=[anywhere, anywhere, scalars, anywhere, scalars, scalars, anywhere, anywhere],
            out_specs=(anywhere, vector, vector),
            scratch_shapes=scratch,
            compiler_params=pltpu.CompilerParams(collective_id=0, has_side_effects=True),
        )(observed, inverse_variance, sed, morph, foot_block, gamma, row_kernel, col_kernel)

    in_specs = (
        P(None, "ty", "tx"),
        P(None, "ty", "tx"),
        P("ty", "tx", None),
        P("ty", "tx", None, None),
        P("ty", "tx"),
        P("ty", "tx"),
        P(),
        P(),
    )
    out_specs = (P(None, "ty", "tx"), P("ty", "tx", None, None), P("ty", "tx", None))
    return jax.shard_map(body, mesh=mesh, in_specs=in_specs, out_specs=out_specs, check_vma=False)
```

time: 316 us -> 73.3 us (0.23)
  the two profiles are of different devices: /device:TPU:96 before, /device:TPU:1 now
where the time goes in v1:
time: 73.3 us; the launch traced here: 73.1 us
  Pallas kernels  67.8 us (92%)
  local copies, waits for them, and re-layouts  3.3 us (5%)
  between operations  1.94 us (3%)
    pallas_call x1, Pallas kernels, body(): pl.pallas_call(functools.partial(kernel, nty, ntx, bands, taps), out_shap...  67.8 us
    unnamed x7, local copies, waits for them, and re-layouts  3.3 us

profile of v1, /device:TPU:1, one launch (start us, length us, event | category | flops | bytes accessed | tf_op | source)
XLA Modules:
  0.0 73.1 jit_solution(1042563735993999865)
XLA Ops:
  1.9 67.8 %shard_map.103 = (f32[6,128,256]{2,1,0:T(8,128)}, f32[1,1,128,128]{3,2,1,0:T(8,128)}, f32[1,1,6]{2,1,0:T(1,128)}) custom-call(f32[6,128,256]{2,1,0:T(8,128)} %obs_hbm.1, f32[6,128,256]{2,1,0:T(8,128)} %iv_hbm.1, f32[1,1,6]{2,1,0:T(1,128)} %sed_s.1, f32[1,1,128,128]{3,2,1,0:T(8,128)} %morph_hbm.1, s32[1,1]{1,0:T(1,128)S(6)} %copy.14.foot_s, ...), custom_call_target="tpu_custom_call" | custom-call | tf_op jit(solution)/shard_map/pallas_call | solution.py:465
  69.8 0.0 copy-start
  69.8 2.1 %copy.16 = f32[6,128,256]{2,1,0:T(8,128)} copy(f32[6,128,256]{2,1,0:T(8,128)} %get-tuple-element.6) | data formatting | bytes 1572864
  71.9 0.0 copy-done
  71.9 0.0 copy-start.1
  71.9 0.6 copy.17
  72.5 0.0 copy-done.1
  72.6 0.5 copy.18
Async XLA Ops:
  69.8 2.1 %copy-start = (f32[1,1,128,128]{3,2,1,0:T(8,128)S(1)}, f32[1,1,128,128]{3,2,1,0:T(8,128)}, u32[]{:S(2)}) copy-start(f32[1,1,128,128]{3,2,1,0:T(8,128)} %get-tuple-element.7) | copy-start | bytes 196612
  71.9 0.7 copy-start.1

commit v2 on v1

--- a/solution.py
+++ b/solution.py
@@ -40,12 +40,14 @@
 
 def kernel(
     nty, ntx, bands, taps,
-    obs_hbm, iv_hbm, sed_s, morph_hbm, foot_s, gamma_s, rk_hbm, ck_hbm,
+    obs_hbm, iv_hbm, sed_hbm, morph_hbm, foot_hbm, gamma_hbm, rk_hbm, ck_hbm,
     resid_hbm, nmorph_ref, nsed_ref,
-    obs_e, iv_e, res_e, model_e, west1, east1, west2, east2, sw1, se1, sw2, se2,
-    morph_v, ob1, ib1, ob2, ib2, ob3, ib3, ob4, ib4, sg_send, sg_in,
+    obs_e, iv_e, res_e, model_e, mixed_e, back, grad,
+    west1, east1, west2, east2, sw1, se1, sw2, se2, pack, edges,
+    morph_v, sed_v, foot_v, gamma_v, info_v,
+    ob1, ib1, ob2, ib2, ob3, ib3, ob4, ib4, sg_send, sg_in,
     slots, sinfo, nslots, sslots, ninfo, soinfo, grads, sgacc,
-    wtab, mtab, rk_v, ck_v, ktab_c, ktab_r, tcol, trow1, trow2, ext_h, ext_l,
+    wtab, mtab, rk_v, ck_v, ktab_c, ktab_r, tcol, trow1, trow2, diag, last, ext_h, ext_l,
     loc_sem, send_sem, a2a_sem, obs_sem, sl_sem, st_sem,
 ):
     ti = lax.axis_index("ty")
@@ -60,13 +62,13 @@
 
     barrier = pltpu.get_barrier_semaphore()
 
-    def greet(j, carry):
-        pl.semaphore_signal(
-            barrier, inc=1, device_id=(ti, lax.rem(me + j, ntx)), device_id_type=MESH
-        )
-        return carry
-
-    lax.fori_loop(1, ntx, greet, 0)
+    def wrapped(j):
+        p = me + j
+        return jnp.where(p >= ntx, p - ntx, p)
+
+    order = sorted(range(1, ntx), key=lambda j: -min(j, ntx - j))
+    for j in order:
+        pl.semaphore_signal(barrier, inc=1, device_id=(ti, wrapped(j)), device_id_type=MESH)
     for yy in (north, south):
         for xx in (me, west, east):
             pl.semaphore_signal(barrier, inc=1, device_id=(yy, xx), device_id_type=MESH)
@@ -76,40 +78,44 @@
     load_ck = pltpu.make_async_copy(ck_hbm, ck_v, loc_sem.at[2])
     load_obs = pltpu.make_async_copy(obs_hbm, obs_e.at[:, HALO : HALO + BOX, :], loc_sem.at[3])
     load_iv = pltpu.make_async_copy(iv_hbm, iv_e.at[:, HALO : HALO + BOX, :], loc_sem.at[4])
+    scalars = [
+        pltpu.make_async_copy(src, dst, loc_sem.at[6 + n])
+        for n, (src, dst) in enumerate(((sed_hbm, sed_v), (foot_hbm, foot_v), (gamma_hbm, gamma_v)))
+    ]
+    for copy in scalars:
+        copy.start()
     load_morph.start()
     load_rk.start()
     load_ck.start()
     load_obs.start()
     load_iv.start()
 
-    foot = foot_s[0, 0]
-    tile = foot // 2
-    box = foot - 2 * tile
-    lane1 = iota((1, BOX), 1)
-    info = jnp.zeros((1, BOX), F32)
-    for b in range(bands):
-        info = jnp.where(lane1 == b, sed_s[0, 0, b], info)
-    info = jnp.where(lane1 == 6, tile.astype(F32), info)
-    info = jnp.where(lane1 == 7, box.astype(F32), info)
     ob1[...] = jnp.zeros_like(ob1)
     ob4[...] = jnp.zeros_like(ob4)
+    lane1 = iota((1, BOX), 1)
+    info_v[...] = jnp.zeros_like(info_v)
+    for copy in scalars:
+        copy.wait()
+    tile = foot_v[...] // 2
+    box = foot_v[...] - 2 * tile
+    info_v[0:1, 0:bands] = sed_v[0]
+    info = info_v[0:1, :]
+    own_tile = tile.astype(F32)
+    info = jnp.where(lane1 == 6, own_tile, info)
+    info = jnp.where(lane1 == 7, box.astype(F32), info)
     ob1[pl.ds(rows, ntx, stride=m1), :] = jnp.broadcast_to(info, (ntx, BOX))
     load_morph.wait()
     for r in range(rows):
         ob1[pl.ds(r, ntx, stride=m1), :] = morph_v[pl.ds(r, ntx, stride=rows), :]
 
     def exchange(out, arrived, m, phase):
-        def step(j, carry):
-            p = lax.rem(me + j, ntx)
+        for j in order:
             pltpu.make_async_remote_copy(
-                out.at[pl.ds(pl.multiple_of(p * m, 8), m)],
+                out.at[pl.ds(pl.multiple_of(wrapped(j) * m, 8), m)],
                 arrived.at[pl.ds(pl.multiple_of(me * m, 8), m)],
                 send_sem.at[phase], a2a_sem.at[phase],
-                device_id=(ti, p), device_id_type=MESH,
+                device_id=(ti, wrapped(j)), device_id_type=MESH,
             ).start()
-            return carry
-
-        lax.fori_loop(1, ntx, step, 0)
         mine = pl.ds(pl.multiple_of(me * m, 8), m)
         arrived[mine, :] = out[mine, :]
 
@@ -153,18 +159,12 @@
             table[st, 1, :, 0:BOX] = full - hi
 
     def band_tables(st, b):
-        strip_row = iota((BOX, NAR), 0)
-        inside = (strip_row >= reach * b) & (strip_row < reach * b + reach)
         for part in range(2):
             spread = jnp.broadcast_to(ktab_c[st, part, pl.ds(b, 1), :], (BOX, WIDE))
             skew = pltpu.roll(spread, 0, 1, stride=1, stride_axis=0)
             for n in range(2):
                 own = pltpu.roll(skew, (WIDE - reach + n * BOX) % WIDE, 1)[:, 0:NAR]
                 tcol[st, b, part, n * BOX : (n + 1) * BOX, :] = own.astype(BF16)
-            for n, shift in enumerate((WIDE - 2 * reach, NAR - reach)):
-                side = pltpu.roll(skew, shift - reach * b, 1)[:, 0:NAR]
-                side = jnp.where(inside, side, 0.0).astype(BF16)
-                tcol[st, b, part, NAR + n * BOX : NAR + (n + 1) * BOX, :] = side
             spread = jnp.broadcast_to(ktab_r[st, part, pl.ds(b, 1), :], (BOX, NAR))
             skew = pltpu.roll(spread, 0, 1, stride=1, stride_axis=0)
             out, trow = ((ext2, trow1), (BOX, trow2))[st]
@@ -173,8 +173,33 @@
                 own = pltpu.roll(skew, (HALO - reach + n) % NAR, 1)
                 trow[b, part, n : n + count] = own[0:count, 0 : trow.shape[3]].astype(BF16)
 
+    tile_row_i, tile_lane = iota((BOX, BOX), 0), iota((BOX, BOX), 1)
+
+    def of_band(index, b):
+        return (index >= reach * b) & (index < reach * b + reach)
+
+    def strip_tables(st):
+        together = tile_row_i < 0
+        for b in range(bands):
+            together = together | (of_band(tile_row_i, b) & of_band(tile_lane, b))
+        rows_i = iota((BOX, WIDE), 0)
+        for part in range(2):
+            spread = jnp.zeros((BOX, WIDE), F32)
+            for b in range(bands):
+                line = jnp.broadcast_to(ktab_c[st, part, b : b + 1, :], (BOX, WIDE))
+                spread = jnp.where(of_band(rows_i, b), line, spread)
+            skew = pltpu.roll(spread, 0, 1, stride=1, stride_axis=0)
+            left = pltpu.roll(skew, WIDE - 2 * reach, 1)
+            empty = jnp.zeros((BOX, BOX), BF16)
+            for n, values in enumerate((left, skew)):
+                block = jnp.where(together, values[:, 0:BOX], 0.0).astype(BF16)
+                at = slice(n * BOX, (n + 1) * BOX)
+                diag[st, part, at, at] = block
+                diag[st, part, at, slice((1 - n) * BOX, (2 - n) * BOX)] = empty
+
     for b in range(bands):
         band_tables(0, b)
+    strip_tables(0)
 
     whole(ob1, ib1, m1, 0).wait_recv()
     infos = ib1[pl.ds(rows, ntx, stride=m1), :]
@@ -215,7 +240,6 @@
         ],
         axis=1,
     )
-    own_tile = tile.astype(F32)
     own_slot = jnp.sum(
         jnp.where(row_i[:, 0:1] == me, slot_col[:, 0:1], 0.0), axis=0, keepdims=True
     )
@@ -236,6 +260,7 @@
     tables(1, sinfo, 1.0)
     for b in range(bands):
         band_tables(1, b)
+    strip_tables(1)
 
     whole(ob2, ib2, m2, 1).wait_recv()
     for s in range(2):
@@ -255,12 +280,11 @@
 
     sw1[...] = jnp.zeros_like(sw1)
     se1[...] = jnp.zeros_like(se1)
-    tile_lane = iota((BOX, BOX), 1)
     for b in range(bands):
         for j in range(2):
             part = sum(wtab[1, s, j, pl.ds(b, 1), :] * slots[s] for s in range(2))
             model_e[b, deep : deep + BOX, j * BOX : (j + 1) * BOX] = part
-            keep = (tile_lane >= reach * b) & (tile_lane < reach * b + reach)
+            keep = of_band(tile_lane, b)
             shift = (reach * b) if j == 0 else (reach * b + reach) % BOX
             moved = pltpu.roll(part, shift, 1) if shift else part
             ref = (sw1, se1)[j]
@@ -277,16 +301,48 @@
     ):
         waits.append(send(src, dst, sl_sem.at[0, 4 + n], sl_sem.at[1, 4 + n], yy, xx))
 
+    def three(hi, lo, right_hi, right_lo):
+        return dot(hi, right_hi) + (dot(hi, right_lo) + dot(lo, right_hi))
+
+    def columns(st, b, image):
+        hi, lo = split(image)
+        return three(hi, lo, tcol[st, b, 0], tcol[st, b, 1])
+
+    def along_rows(trow, b, image):
+        hi, lo = split(image)
+        return three(trow[b, 0], trow[b, 1], hi, lo)
+
+    def own_columns(b, carry):
+        mixed_e[b, deep : deep + BOX] = columns(0, b, model_e[b, deep : deep + BOX])
+        return carry
+
+    lax.fori_loop(0, bands, own_columns, 0)
+
     for copy in waits[0:4]:
         copy.wait_recv()
     tables(0, ninfo, jnp.where(ti > 0, 1.0, 0.0))
     tables(2, soinfo, jnp.where(ti < nty - 1, 1.0, 0.0))
 
-    for b in range(bands):
-        for which, ref, start in ((0, nslots, 0), (2, sslots, deep + BOX)):
-            for j in range(2):
-                part = sum(wtab[which, s, j, pl.ds(b, 1), :] * ref[s] for s in range(2))
-                model_e[b, start : start + deep, j * BOX : (j + 1) * BOX] = part
+    def outer_columns(b, carry):
+        image = jnp.concatenate(
+            [
+                jnp.concatenate(
+                    [
+                        sum(wtab[which, s, j, pl.ds(b, 1), :] * ref[s] for s in range(2))
+                        for j in range(2)
+                    ],
+                    axis=1,
+                )
+                for which, ref in ((0, nslots), (2, sslots))
+            ],
+            axis=0,
+        )
+        image = columns(0, b, image)
+        mixed_e[b, 0:deep] = image[0:deep]
+        mixed_e[b, deep + BOX : ext1] = image[deep:]
+        return carry
+
+    lax.fori_loop(0, bands, outer_columns, 0)
 
     load_obs.wait()
     load_iv.wait()
@@ -303,29 +359,29 @@
             ext_h[0:count, n * BOX : (n + 1) * BOX] = hi
             ext_l[0:count, n * BOX : (n + 1) * BOX] = lo
 
-    def passes(st, b, image, count, trow):
-        hi, lo = split(image)
-        hi = jnp.concatenate([hi, ext_h[0:count, :]], axis=1)
-        lo = jnp.concatenate([lo, ext_l[0:count, :]], axis=1)
-        mixed = dot(hi, tcol[st, b, 0]) + (dot(hi, tcol[st, b, 1]) + dot(lo, tcol[st, b, 0]))
-        hi, lo = split(mixed)
-        return dot(trow[b, 0], hi) + (dot(trow[b, 0], lo) + dot(trow[b, 1], hi))
-
     halo_parts(west1, east1, ext1, deep)
+    pack[...] = three(ext_h[...], ext_l[...], diag[0, 0], diag[0, 1])
     sw2[...] = jnp.zeros_like(sw2)
     se2[...] = jnp.zeros_like(se2)
     row = iota((ext2, 2 * BOX), 0)
     inside = ((row >= HALO) | (ti > 0)) & ((row < HALO + BOX) | (ti < nty - 1))
-    lane = iota((ext2, BOX), 1)
+    first_lanes = iota((ext1, BOX), 1) < reach
+    last_lanes = iota((ext1, BOX), 1) >= BOX - reach
 
     def first(b, carry):
-        predicted = passes(0, b, model_e[b], ext1, trow1)
+        left = pltpu.roll(pack[:, 0:BOX], lax.rem(BOX - reach * b, BOX), 1)
+        left = mixed_e[b, :, 0:BOX] + jnp.where(first_lanes, left, 0.0)
+        right = pltpu.roll(pack[:, BOX:], lax.rem(2 * BOX - reach - reach * b, BOX), 1)
+        right = mixed_e[b, :, BOX:] + jnp.where(last_lanes, right, 0.0)
+        predicted = along_rows(trow1, b, jnp.concatenate([left, right], axis=1))
         residual = jnp.where(inside, iv_e[b] * (obs_e[b] - predicted), 0.0)
         res_e[b] = residual
-        keep = (lane >= reach * b) & (lane < reach * b + reach)
-        moved = pltpu.roll(residual[:, 0:BOX], reach * b, 1)
+        image = along_rows(trow2, b, residual)
+        back[b] = image
+        keep = of_band(tile_lane, b)
+        moved = pltpu.roll(image[:, 0:BOX], reach * b, 1)
         sw2[...] = jnp.where(keep, moved, sw2[...])
-        moved = pltpu.roll(residual[:, BOX:], lax.rem(reach * b + reach, BOX), 1)
+        moved = pltpu.roll(image[:, BOX:], lax.rem(reach * b + reach, BOX), 1)
         se2[...] = jnp.where(keep, moved, se2[...])
         return carry
 
@@ -336,27 +392,66 @@
     ]
     store = pltpu.make_async_copy(res_e.at[:, HALO : HALO + BOX, :], resid_hbm, loc_sem.at[5])
     store.start()
+
+    for side in range(2):
+        at = slice(side * BOX, (side + 1) * BOX)
+        full = diag[1, 0, at, at].astype(F32) + diag[1, 1, at, at].astype(F32)
+        fold = jnp.zeros((BOX, BOX), F32)
+        for b in range(bands):
+            here_lane = tile_lane if side == 0 else tile_lane - (BOX - reach)
+            inside_lane = (here_lane >= 0) & (here_lane < reach)
+            fold = jnp.where(inside_lane & (tile_row_i - reach * b == here_lane), 1.0, fold)
+        fold = fold.astype(BF16)
+        for s in range(2):
+            weight = jnp.zeros((1, BOX), F32)
+            for b in range(bands):
+                weight = jnp.where(of_band(lane1, b), wtab[1, s, side, b : b + 1, :], weight)
+            hi, lo = split(full * weight)
+            hi, lo = split(dot(hi, fold) + dot(lo, fold))
+            last[0, at, s * BOX : (s + 1) * BOX] = hi
+            last[1, at, s * BOX : (s + 1) * BOX] = lo
+
     grads[...] = jnp.zeros_like(grads)
-    sgacc[...] = jnp.zeros_like(sgacc)
-    for copy in strips:
-        copy.wait_recv()
-    halo_parts(west2, east2, ext2, HALO)
 
     def second(b, carry):
-        gradient = passes(1, b, res_e[b], ext2, trow2)
+        gradient = columns(1, b, back[b])
+        grad[b] = gradient
         halves = (gradient[:, 0:BOX], gradient[:, BOX:])
         for s in range(2):
             grads[s] += sum(wtab[1, s, j, pl.ds(b, 1), :] * halves[j] for j in range(2))
-            under = sum(mtab[s, j, pl.ds(b, 1), :] * halves[j] for j in range(2))
-            sgacc[s, pl.ds(b, 1), :] = jnp.sum(slots[s] * under, axis=0, keepdims=True)
         return carry
 
     lax.fori_loop(0, bands, second, 0)
+    for copy in strips:
+        copy.wait_recv()
+    for n, (ref, ok) in enumerate(((west2, me > 0), (east2, me < ntx - 1))):
+        hi, lo = split(jnp.where(ok, ref[...], 0.0))
+        ext_h[0:BOX, n * BOX : (n + 1) * BOX] = hi
+        ext_l[0:BOX, n * BOX : (n + 1) * BOX] = lo
+    share = three(ext_h[0:BOX], ext_l[0:BOX], last[0], last[1])
+    for s in range(2):
+        grads[s] += share[:, s * BOX : (s + 1) * BOX]
 
     for s in range(2):
         for r in range(rows):
             ob3[pl.ds(s * rows + r, ntx, stride=m2), :] = grads[s, pl.ds(r, ntx, stride=rows), :]
     exchange(ob3, ib3, m2, 2)
+    edges[...] = three(ext_h[0:BOX], ext_l[0:BOX], diag[1, 0], diag[1, 1])
+    sgacc[...] = jnp.zeros_like(sgacc)
+
+    def spectra(b, carry):
+        left = pltpu.roll(edges[:, 0:BOX], lax.rem(BOX - reach * b, BOX), 1)
+        right = pltpu.roll(edges[:, BOX:], lax.rem(2 * BOX - reach - reach * b, BOX), 1)
+        halves = (
+            grad[b, :, 0:BOX] + jnp.where(tile_lane < reach, left, 0.0),
+            grad[b, :, BOX:] + jnp.where(tile_lane >= BOX - reach, right, 0.0),
+        )
+        for s in range(2):
+            under = sum(mtab[s, j, pl.ds(b, 1), :] * halves[j] for j in range(2))
+            sgacc[s, pl.ds(b, 1), :] = jnp.sum(slots[s] * under, axis=0, keepdims=True)
+        return carry
+
+    lax.fori_loop(0, bands, spectra, 0)
     line = jnp.zeros((1, BOX), F32)
     for s in range(2):
         column = jnp.broadcast_to(jnp.sum(sgacc[s], axis=1, keepdims=True), (8, BOX))
@@ -365,15 +460,11 @@
     sg_send[0] = line
     sg_in[me] = line
 
-    def spread_sed(j, carry):
-        p = lax.rem(me + j, ntx)
+    for j in order:
         pltpu.make_async_remote_copy(
             sg_send.at[0], sg_in.at[me], send_sem.at[4], a2a_sem.at[4],
-            device_id=(ti, p), device_id_type=MESH,
+            device_id=(ti, wrapped(j)), device_id_type=MESH,
         ).start()
-        return carry
-
-    lax.fori_loop(1, ntx, spread_sed, 0)
 
     whole(ob3, ib3, m2, 2).wait_recv()
     pieces = jnp.concatenate(
@@ -391,10 +482,10 @@
     exchange(ob4, ib4, m4, 3)
 
     square = jnp.sum(jnp.where(lane1 < bands, info * info, 0.0), axis=1, keepdims=True)
-    step_morph = gamma_s[0, 0] / square
+    step_morph = gamma_v[...] / square
     full = morph_v[...]
     norm = jnp.sum(jnp.sum(full * full, axis=0, keepdims=True), axis=1, keepdims=True)
-    step_sed = gamma_s[0, 0] / jnp.sqrt(norm)
+    step_sed = gamma_v[...] / jnp.sqrt(norm)
 
     part = pl.ds(0, ntx - 1)
     seds = pltpu.make_async_remote_copy(
@@ -424,6 +515,21 @@
     store.wait()
 
 
+def write_out(resid, morph, sed, resid_o, morph_o, sed_o, resid_v, morph_v, sed_v, in_sem, out_sem):
+    bands = resid.shape[0]
+    trips = [(resid.at[b], resid_v.at[b], resid_o.at[b]) for b in range(bands)]
+    trips += [(morph, morph_v, morph_o), (sed, sed_v, sed_o)]
+    loads = [pltpu.make_async_copy(a, v, in_sem.at[n]) for n, (a, v, _) in enumerate(trips)]
+    stores = [pltpu.make_async_copy(v, o, out_sem.at[n]) for n, (_, v, o) in enumerate(trips)]
+    for copy in loads:
+        copy.start()
+    for load, out in zip(loads, stores):
+        load.wait()
+        out.start()
+    for copy in stores:
+        copy.wait()
+
+
 def solution(mesh):
     nty, ntx = mesh.shape["ty"], mesh.shape["tx"]
 
@@ -440,10 +546,12 @@
 
         scratch = [
             vmem(bands, ext2, width), vmem(bands, ext2, width), vmem(bands, ext2, width),
-            vmem(bands, ext1, width),
-            vmem(ext1, BOX), vmem(ext1, BOX), vmem(ext2, BOX), vmem(ext2, BOX),
-            vmem(BOX, BOX), vmem(BOX, BOX), vmem(ext2, BOX), vmem(ext2, BOX),
-            vmem(BOX, BOX),
+            vmem(bands, ext1, width), vmem(bands, ext1, width),
+            vmem(bands, height, width), vmem(bands, height, width),
+            vmem(ext1, BOX), vmem(ext1, BOX), vmem(BOX, BOX), vmem(BOX, BOX),
+            vmem(BOX, BOX), vmem(BOX, BOX), vmem(BOX, BOX), vmem(BOX, BOX),
+            vmem(ext1, NAR), vmem(BOX, NAR),
+            vmem(BOX, BOX), vmem(*sed.shape), vmem(1, 1, dtype=jnp.int32), vmem(1, 1), vmem(8, BOX),
             vmem(ntx * m1, BOX), vmem(ntx * m1, BOX), vmem(ntx * m2, BOX), vmem(ntx * m2, BOX),
             vmem(ntx * m2, BOX), vmem(ntx * m2, BOX), vmem(ntx * m4, BOX), vmem(ntx * m4, BOX),
             vmem(1, 1, BOX), vmem(ntx, 1, BOX),
@@ -452,28 +560,37 @@
             vmem(3, 2, 2, 8, BOX), vmem(2, 2, 8, BOX),
             vmem(bands, taps), vmem(bands, taps),
             vmem(2, 2, 8, WIDE), vmem(2, 2, 8, NAR),
-            vmem(2, bands, 2, 2 * NAR, NAR, dtype=BF16),
+            vmem(2, bands, 2, NAR, NAR, dtype=BF16),
             vmem(bands, 2, ext2, ext1, dtype=BF16), vmem(bands, 2, BOX, ext2, dtype=BF16),
+            vmem(2, 2, NAR, NAR, dtype=BF16), vmem(2, NAR, NAR, dtype=BF16),
             vmem(ext1, NAR, dtype=BF16), vmem(ext1, NAR, dtype=BF16),
-            pltpu.SemaphoreType.DMA((6,)), pltpu.SemaphoreType.DMA((5,)),
+            pltpu.SemaphoreType.DMA((9,)), pltpu.SemaphoreType.DMA((5,)),
             pltpu.SemaphoreType.DMA((5,)), pltpu.SemaphoreType.DMA((2, 4)),
             pltpu.SemaphoreType.DMA((2, 10)), pltpu.SemaphoreType.DMA((2, 2)),
         ]
         anywhere = pl.BlockSpec(memory_space=pl.ANY)
-        scalars = pl.BlockSpec(memory_space=pltpu.SMEM)
         vector = pl.BlockSpec(memory_space=pltpu.VMEM)
-        return pl.pallas_call(
+        shapes = tuple(
+            jax.ShapeDtypeStruct(a.shape, F32) for a in (observed, morph, sed)
+        )
+        results = pl.pallas_call(
             functools.partial(kernel, nty, ntx, bands, taps),
-            out_shape=(
-                jax.ShapeDtypeStruct(observed.shape, F32),
-                jax.ShapeDtypeStruct(morph.shape, F32),
-                jax.ShapeDtypeStruct(sed.shape, F32),
-            ),
-            in_specs=[anywhere, anywhere, scalars, anywhere, scalars, scalars, anywhere, anywhere],
+            out_shape=shapes,
+            in_specs=[pl.BlockSpec(memory_space=pltpu.HBM)] * 8,
             out_specs=(anywhere, vector, vector),
             scratch_shapes=scratch,
             compiler_params=pltpu.CompilerParams(collective_id=0, has_side_effects=True),
         )(observed, inverse_variance, sed, morph, foot_block, gamma, row_kernel, col_kernel)
+        return pl.pallas_call(
+            write_out,
+            out_shape=shapes,
+            in_specs=[anywhere] * 3,
+            out_specs=(anywhere,) * 3,
+            scratch_shapes=[
+                vmem(bands, height, width), vmem(*morph.shape), vmem(*sed.shape),
+                pltpu.SemaphoreType.DMA((bands + 2,)), pltpu.SemaphoreType.DMA((bands + 2,)),
+            ],
+        )(*results)
 
     in_specs = (
         P(None, "ty", "tx"),

time: 73.3 us -> 65.9 us (0.90)
  Pallas kernels: 67.8 us -> 63.8 us
  local copies, waits for them, and re-layouts: 3.3 us -> 0 us
    pallas_call x1, Pallas kernels: 67.8 us -> 61.8 us  [body(): pl.pallas_call(functools.partial(kernel, nty, ntx, bands, taps), out_shap...]
    unnamed x7 -> x0, local copies, waits for them, and re-layouts: 3.3 us -> none
    pallas_call x0 -> x1, Pallas kernels: none -> 2.02 us  [body(): pl.pallas_call(write_out, out_shape=shapes, in_specs=[anywhere] * 3, out_...]
where the time goes in v2:
time: 65.9 us; the launch traced here: 65.7 us
  Pallas kernels  63.8 us (97%)
  between operations  1.93 us (3%)
    pallas_call x1, Pallas kernels, body(): pl.pallas_call(functools.partial(kernel, nty, ntx, bands, taps), out_shap...  61.8 us
    pallas_call x1, Pallas kernels, body(): pl.pallas_call(write_out, out_shape=shapes, in_specs=[anywhere] * 3, out_...  2.02 us

profile of v2, /device:TPU:1, one launch (start us, length us, event | category | flops | bytes accessed | tf_op | source)
XLA Modules:
  0.0 65.7 jit_solution(15889238250079457062)
XLA Ops:
  1.9 61.8 %shard_map.103 = (f32[6,128,256]{2,1,0:T(8,128)}, f32[1,1,128,128]{3,2,1,0:T(8,128)}, f32[1,1,6]{2,1,0:T(1,128)}) custom-call(f32[6,128,256]{2,1,0:T(8,128)} %obs_hbm.1, f32[6,128,256]{2,1,0:T(8,128)} %iv_hbm.1, f32[1,1,6]{2,1,0:T(1,128)} %sed_hbm.1, f32[1,1,128,128]{3,2,1,0:T(8,128)} %morph_hbm.1, s32[1,1]{1,0:T(1,128)S(6)} %copy.11.foot_hbm, ...), custom_call_target="tpu_custom_call" | custom-call | tf_op jit(solution)/shard_map/pallas_call | solution.py:576
  63.7 2.0 %shard_map.104 = (f32[6,128,256]{2,1,0:T(8,128)}, f32[1,1,128,128]{3,2,1,0:T(8,128)}, f32[1,1,6]{2,1,0:T(1,128)}) custom-call(f32[6,128,256]{2,1,0:T(8,128)} %get-tuple-element.6.resid, f32[1,1,128,128]{3,2,1,0:T(8,128)} %get-tuple-element.7.morph, f32[1,1,6]{2,1,0:T(1,128)} %get-tuple-element.8.sed), custom_call_target="tpu_custom_call" | custom-call | tf_op jit(solution)/shard_map/pallas_call | solution.py:584

commit v3 on v2

--- a/solution.py
+++ b/solution.py
@@ -17,10 +17,6 @@
 NAR = 256
 
 
-def up8(n):
-    return (n + 7) // 8 * 8
-
-
 def iota(shape, dim):
     return lax.broadcasted_iota(jnp.int32, shape, dim)
 
@@ -41,10 +37,10 @@
 def kernel(
     nty, ntx, bands, taps,
     obs_hbm, iv_hbm, sed_hbm, morph_hbm, foot_hbm, gamma_hbm, rk_hbm, ck_hbm,
-    resid_hbm, nmorph_ref, nsed_ref,
-    obs_e, iv_e, res_e, model_e, mixed_e, back, grad,
+    resid_ref, nmorph_ref, nsed_ref,
+    obs_e, iv_e, model_e, mixed_e, back, grad,
     west1, east1, west2, east2, sw1, se1, sw2, se2, pack, edges,
-    morph_v, sed_v, foot_v, gamma_v, info_v,
+    morph_v, sed_v, foot_v, gamma_v, info_v, info_send, info_in,
     ob1, ib1, ob2, ib2, ob3, ib3, ob4, ib4, sg_send, sg_in,
     slots, sinfo, nslots, sslots, ninfo, soinfo, grads, sgacc,
     wtab, mtab, rk_v, ck_v, ktab_c, ktab_r, tcol, trow1, trow2, diag, last, ext_h, ext_l,
@@ -54,7 +50,6 @@
     me = lax.axis_index("tx")
     reach = (taps - 1) // 2
     rows = BOX // ntx
-    m1, m2, m4 = up8(rows + 1), 2 * rows, up8(rows)
     deep = 2 * HALO
     ext1, ext2 = BOX + 2 * deep, BOX + 2 * HALO
     north, south = lax.rem(ti + nty - 1, nty), lax.rem(ti + 1, nty)
@@ -90,8 +85,6 @@
     load_obs.start()
     load_iv.start()
 
-    ob1[...] = jnp.zeros_like(ob1)
-    ob4[...] = jnp.zeros_like(ob4)
     lane1 = iota((1, BOX), 1)
     info_v[...] = jnp.zeros_like(info_v)
     for copy in scalars:
@@ -103,31 +96,34 @@
     own_tile = tile.astype(F32)
     info = jnp.where(lane1 == 6, own_tile, info)
     info = jnp.where(lane1 == 7, box.astype(F32), info)
-    ob1[pl.ds(rows, ntx, stride=m1), :] = jnp.broadcast_to(info, (ntx, BOX))
+    info_send[0] = info
     load_morph.wait()
     for r in range(rows):
-        ob1[pl.ds(r, ntx, stride=m1), :] = morph_v[pl.ds(r, ntx, stride=rows), :]
-
-    def exchange(out, arrived, m, phase):
+        ob1[:, r, :] = morph_v[pl.ds(r, ntx, stride=rows), :]
+
+    def copy_to(src, dst, phase, p):
+        return pltpu.make_async_remote_copy(
+            src, dst, send_sem.at[phase], a2a_sem.at[phase],
+            device_id=(ti, p), device_id_type=MESH,
+        )
+
+    def exchange(out, arrived, phase):
         for j in order:
-            pltpu.make_async_remote_copy(
-                out.at[pl.ds(pl.multiple_of(wrapped(j) * m, 8), m)],
-                arrived.at[pl.ds(pl.multiple_of(me * m, 8), m)],
-                send_sem.at[phase], a2a_sem.at[phase],
-                device_id=(ti, wrapped(j)), device_id_type=MESH,
-            ).start()
-        mine = pl.ds(pl.multiple_of(me * m, 8), m)
-        arrived[mine, :] = out[mine, :]
-
-    def whole(out, arrived, m, phase):
-        part = pl.ds(0, (ntx - 1) * m)
-        return pltpu.make_async_remote_copy(
-            out.at[part], arrived.at[part], send_sem.at[phase], a2a_sem.at[phase],
-            device_id=(ti, east), device_id_type=MESH,
-        )
+            copy_to(out.at[wrapped(j)], arrived.at[me], phase, wrapped(j)).start()
+        arrived[me] = out[me]
+
+    def spread(out, arrived, phase):
+        for j in order:
+            copy_to(out.at[0], arrived.at[me], phase, wrapped(j)).start()
+        arrived[me] = out[0]
+
+    def whole(arrived, phase):
+        part = arrived.at[pl.ds(0, ntx - 1)]
+        return copy_to(part, part, phase, east)
 
     pl.semaphore_wait(barrier, ntx - 1 + 6)
-    exchange(ob1, ib1, m1, 0)
+    spread(info_send, info_in, 5)
+    exchange(ob1, ib1, 0)
 
     def send(src, dst, s_sem, r_sem, yy, xx):
         copy = pltpu.make_async_remote_copy(
@@ -201,8 +197,9 @@
         band_tables(0, b)
     strip_tables(0)
 
-    whole(ob1, ib1, m1, 0).wait_recv()
-    infos = ib1[pl.ds(rows, ntx, stride=m1), :]
+    whole(info_in, 5).wait_recv()
+    whole(ib1, 0).wait_recv()
+    infos = info_in[:, 0, :]
     wide = (ntx, BOX)
     row_i, lane_i = iota(wide, 0), iota(wide, 1)
     tile_col = jnp.broadcast_to(infos[:, 6:7], wide)
@@ -218,14 +215,14 @@
         jnp.where((tile_row == target) & (slot_row == float(s)), 1.0, 0.0)[:, 0:ntx]
         for s in range(2)
     ]
-    pieces = jnp.concatenate([ib1[pl.ds(r, ntx, stride=m1), :] for r in range(rows)], axis=1)
+    pieces = jnp.concatenate([ib1[:, r, :] for r in range(rows)], axis=1)
     chosen = exact(jnp.concatenate(pick, axis=0), pieces)
     for s in range(2):
         for r in range(rows):
-            ob2[pl.ds(s * rows + r, ntx, stride=m2), :] = chosen[
+            ob2[:, s * rows + r, :] = chosen[
                 s * ntx : (s + 1) * ntx, r * BOX : (r + 1) * BOX
             ]
-    exchange(ob2, ib2, m2, 1)
+    exchange(ob2, ib2, 1)
 
     here = me.astype(F32)
     for s in range(2):
@@ -262,10 +259,10 @@
         band_tables(1, b)
     strip_tables(1)
 
-    whole(ob2, ib2, m2, 1).wait_recv()
+    whole(ib2, 1).wait_recv()
     for s in range(2):
         for r in range(rows):
-            slots[s, pl.ds(r, ntx, stride=rows), :] = ib2[pl.ds(s * rows + r, ntx, stride=m2), :]
+            slots[s, pl.ds(r, ntx, stride=rows), :] = ib2[:, s * rows + r, :]
 
     waits = []
     for n, (src, dst, yy) in enumerate(
@@ -310,20 +307,19 @@
 
     def along_rows(trow, b, image):
         hi, lo = split(image)
-        return three(trow[b, 0], trow[b, 1], hi, lo)
-
-    def own_columns(b, carry):
+        count, depth = trow.shape[2:]
+        both = dot(trow[b].reshape(2 * count, depth), hi)
+        return both[:count] + (both[count:] + dot(trow[b, 0], lo))
+
+    for b in range(bands):
         mixed_e[b, deep : deep + BOX] = columns(0, b, model_e[b, deep : deep + BOX])
-        return carry
-
-    lax.fori_loop(0, bands, own_columns, 0)
 
     for copy in waits[0:4]:
         copy.wait_recv()
     tables(0, ninfo, jnp.where(ti > 0, 1.0, 0.0))
     tables(2, soinfo, jnp.where(ti < nty - 1, 1.0, 0.0))
 
-    def outer_columns(b, carry):
+    for b in range(bands):
         image = jnp.concatenate(
             [
                 jnp.concatenate(
@@ -340,9 +336,6 @@
         image = columns(0, b, image)
         mixed_e[b, 0:deep] = image[0:deep]
         mixed_e[b, deep + BOX : ext1] = image[deep:]
-        return carry
-
-    lax.fori_loop(0, bands, outer_columns, 0)
 
     load_obs.wait()
     load_iv.wait()
@@ -361,38 +354,32 @@
 
     halo_parts(west1, east1, ext1, deep)
     pack[...] = three(ext_h[...], ext_l[...], diag[0, 0], diag[0, 1])
-    sw2[...] = jnp.zeros_like(sw2)
-    se2[...] = jnp.zeros_like(se2)
     row = iota((ext2, 2 * BOX), 0)
     inside = ((row >= HALO) | (ti > 0)) & ((row < HALO + BOX) | (ti < nty - 1))
     first_lanes = iota((ext1, BOX), 1) < reach
     last_lanes = iota((ext1, BOX), 1) >= BOX - reach
 
-    def first(b, carry):
-        left = pltpu.roll(pack[:, 0:BOX], lax.rem(BOX - reach * b, BOX), 1)
+    to_west = to_east = jnp.zeros((BOX, BOX), F32)
+    for b in range(bands):
+        left = pltpu.roll(pack[:, 0:BOX], (BOX - reach * b) % BOX, 1)
         left = mixed_e[b, :, 0:BOX] + jnp.where(first_lanes, left, 0.0)
-        right = pltpu.roll(pack[:, BOX:], lax.rem(2 * BOX - reach - reach * b, BOX), 1)
+        right = pltpu.roll(pack[:, BOX:], (2 * BOX - reach - reach * b) % BOX, 1)
         right = mixed_e[b, :, BOX:] + jnp.where(last_lanes, right, 0.0)
         predicted = along_rows(trow1, b, jnp.concatenate([left, right], axis=1))
         residual = jnp.where(inside, iv_e[b] * (obs_e[b] - predicted), 0.0)
-        res_e[b] = residual
+        resid_ref[b] = residual[HALO : HALO + BOX]
         image = along_rows(trow2, b, residual)
         back[b] = image
         keep = of_band(tile_lane, b)
-        moved = pltpu.roll(image[:, 0:BOX], reach * b, 1)
-        sw2[...] = jnp.where(keep, moved, sw2[...])
-        moved = pltpu.roll(image[:, BOX:], lax.rem(reach * b + reach, BOX), 1)
-        se2[...] = jnp.where(keep, moved, se2[...])
-        return carry
-
-    lax.fori_loop(0, bands, first, 0)
+        to_west = jnp.where(keep, pltpu.roll(image[:, 0:BOX], reach * b, 1), to_west)
+        moved = pltpu.roll(image[:, BOX:], (reach * b + reach) % BOX, 1)
+        to_east = jnp.where(keep, moved, to_east)
+    sw2[...] = to_west
+    se2[...] = to_east
     strips = [
         send(se2, west2, st_sem.at[0, 0], st_sem.at[1, 0], ti, east),
         send(sw2, east2, st_sem.at[0, 1], st_sem.at[1, 1], ti, west),
     ]
-    store = pltpu.make_async_copy(res_e.at[:, HALO : HALO + BOX, :], resid_hbm, loc_sem.at[5])
-    store.start()
-
     for side in range(2):
         at = slice(side * BOX, (side + 1) * BOX)
         full = diag[1, 0, at, at].astype(F32) + diag[1, 1, at, at].astype(F32)
@@ -411,17 +398,16 @@
             last[0, at, s * BOX : (s + 1) * BOX] = hi
             last[1, at, s * BOX : (s + 1) * BOX] = lo
 
-    grads[...] = jnp.zeros_like(grads)
-
-    def second(b, carry):
+    totals = [jnp.zeros((BOX, BOX), F32) for _ in range(2)]
+    for b in range(bands):
         gradient = columns(1, b, back[b])
         grad[b] = gradient
         halves = (gradient[:, 0:BOX], gradient[:, BOX:])
         for s in range(2):
-            grads[s] += sum(wtab[1, s, j, pl.ds(b, 1), :] * halves[j] for j in range(2))
-        return carry
-
-    lax.fori_loop(0, bands, second, 0)
+            for j in range(2):
+                totals[s] = totals[s] + wtab[1, s, j, b : b + 1, :] * halves[j]
+    for s in range(2):
+        grads[s] = totals[s]
     for copy in strips:
         copy.wait_recv()
     for n, (ref, ok) in enumerate(((west2, me > 0), (east2, me < ntx - 1))):
@@ -434,8 +420,8 @@
 
     for s in range(2):
         for r in range(rows):
-            ob3[pl.ds(s * rows + r, ntx, stride=m2), :] = grads[s, pl.ds(r, ntx, stride=rows), :]
-    exchange(ob3, ib3, m2, 2)
+            ob3[:, s * rows + r, :] = grads[s, pl.ds(r, ntx, stride=rows), :]
+    exchange(ob3, ib3, 2)
     edges[...] = three(ext_h[0:BOX], ext_l[0:BOX], diag[1, 0], diag[1, 1])
     sgacc[...] = jnp.zeros_like(sgacc)
 
@@ -458,19 +444,13 @@
         mark = iota((8, BOX), 1) == iota((8, BOX), 0) + 8 * s
         line = line + jnp.sum(jnp.where(mark, column, 0.0), axis=0, keepdims=True)
     sg_send[0] = line
-    sg_in[me] = line
-
-    for j in order:
-        pltpu.make_async_remote_copy(
-            sg_send.at[0], sg_in.at[me], send_sem.at[4], a2a_sem.at[4],
-            device_id=(ti, wrapped(j)), device_id_type=MESH,
-        ).start()
-
-    whole(ob3, ib3, m2, 2).wait_recv()
+    spread(sg_send, sg_in, 4)
+
+    whole(ib3, 2).wait_recv()
     pieces = jnp.concatenate(
         [
             jnp.concatenate(
-                [ib3[pl.ds(s * rows + r, ntx, stride=m2), :] for r in range(rows)], axis=1
+                [ib3[:, s * rows + r, :] for r in range(rows)], axis=1
             )
             for s in range(2)
         ],
@@ -478,8 +458,8 @@
     )
     chosen = exact(give, pieces)
     for r in range(rows):
-        ob4[pl.ds(r, ntx, stride=m4), :] = chosen[:, r * BOX : (r + 1) * BOX]
-    exchange(ob4, ib4, m4, 3)
+        ob4[:, r, :] = chosen[:, r * BOX : (r + 1) * BOX]
+    exchange(ob4, ib4, 3)
 
     square = jnp.sum(jnp.where(lane1 < bands, info * info, 0.0), axis=1, keepdims=True)
     step_morph = gamma_v[...] / square
@@ -487,45 +467,30 @@
     norm = jnp.sum(jnp.sum(full * full, axis=0, keepdims=True), axis=1, keepdims=True)
     step_sed = gamma_v[...] / jnp.sqrt(norm)
 
-    part = pl.ds(0, ntx - 1)
-    seds = pltpu.make_async_remote_copy(
-        sg_in.at[part], sg_in.at[part], send_sem.at[4], a2a_sem.at[4],
-        device_id=(ti, east), device_id_type=MESH,
-    )
-    seds.wait_recv()
+    whole(sg_in, 4).wait_recv()
     terms = jnp.zeros((1, BOX), F32)
     for d in range(ntx):
         terms = terms + jnp.where(own_tile == float(d), sg_in[d], 0.0)
     terms = jnp.where(own_slot == 0.0, terms, pltpu.roll(terms, BOX - 8, 1))
     nsed_ref[0] = jnp.maximum(info + step_sed * terms, 0.0)[:, 0:bands]
 
-    whole(ob4, ib4, m4, 3).wait_recv()
+    whole(ib4, 3).wait_recv()
     for r in range(rows):
         at = pl.ds(r, ntx, stride=rows)
-        update = step_morph * ib4[pl.ds(r, ntx, stride=m4), :]
+        update = step_morph * ib4[:, r, :]
         nmorph_ref[0, 0, at, :] = jnp.maximum(morph_v[at, :] + update, 0.0)
 
-    whole(ob1, ib1, m1, 0).wait_send()
-    whole(ob2, ib2, m2, 1).wait_send()
-    whole(ob3, ib3, m2, 2).wait_send()
-    whole(ob4, ib4, m4, 3).wait_send()
-    seds.wait_send()
+    for phase, arrived in enumerate((ib1, ib2, ib3, ib4, sg_in, info_in)):
+        whole(arrived, phase).wait_send()
     for copy in images + waits + strips:
         copy.wait_send()
-    store.wait()
-
-
-def write_out(resid, morph, sed, resid_o, morph_o, sed_o, resid_v, morph_v, sed_v, in_sem, out_sem):
-    bands = resid.shape[0]
-    trips = [(resid.at[b], resid_v.at[b], resid_o.at[b]) for b in range(bands)]
-    trips += [(morph, morph_v, morph_o), (sed, sed_v, sed_o)]
-    loads = [pltpu.make_async_copy(a, v, in_sem.at[n]) for n, (a, v, _) in enumerate(trips)]
-    stores = [pltpu.make_async_copy(v, o, out_sem.at[n]) for n, (_, v, o) in enumerate(trips)]
-    for copy in loads:
+
+
+def write_out(resid, morph, sed, resid_o, morph_o, sed_o, sem):
+    pairs = ((resid, resid_o), (morph, morph_o), (sed, sed_o))
+    stores = [pltpu.make_async_copy(a, o, sem.at[n]) for n, (a, o) in enumerate(pairs)]
+    for copy in stores:
         copy.start()
-    for load, out in zip(loads, stores):
-        load.wait()
-        out.start()
     for copy in stores:
         copy.wait()
 
@@ -537,7 +502,6 @@
         bands, height, width = observed.shape
         taps = row_kernel.shape[1]
         rows = BOX // ntx
-        m1, m2, m4 = up8(rows + 1), 2 * rows, up8(rows)
         deep = 2 * HALO
         ext1, ext2 = height + 2 * deep, height + 2 * HALO
 
@@ -545,15 +509,18 @@
             return pltpu.VMEM(shape, dtype)
 
         scratch = [
-            vmem(bands, ext2, width), vmem(bands, ext2, width), vmem(bands, ext2, width),
+            vmem(bands, ext2, width), vmem(bands, ext2, width),
             vmem(bands, ext1, width), vmem(bands, ext1, width),
             vmem(bands, height, width), vmem(bands, height, width),
             vmem(ext1, BOX), vmem(ext1, BOX), vmem(BOX, BOX), vmem(BOX, BOX),
             vmem(BOX, BOX), vmem(BOX, BOX), vmem(BOX, BOX), vmem(BOX, BOX),
             vmem(ext1, NAR), vmem(BOX, NAR),
             vmem(BOX, BOX), vmem(*sed.shape), vmem(1, 1, dtype=jnp.int32), vmem(1, 1), vmem(8, BOX),
-            vmem(ntx * m1, BOX), vmem(ntx * m1, BOX), vmem(ntx * m2, BOX), vmem(ntx * m2, BOX),
-            vmem(ntx * m2, BOX), vmem(ntx * m2, BOX), vmem(ntx * m4, BOX), vmem(ntx * m4, BOX),
+            vmem(1, 1, BOX), vmem(ntx, 1, BOX),
+            vmem(ntx, rows, BOX), vmem(ntx, rows, BOX),
+            vmem(ntx, 2 * rows, BOX), vmem(ntx, 2 * rows, BOX),
+            vmem(ntx, 2 * rows, BOX), vmem(ntx, 2 * rows, BOX),
+            vmem(ntx, rows, BOX), vmem(ntx, rows, BOX),
             vmem(1, 1, BOX), vmem(ntx, 1, BOX),
             vmem(2, BOX, BOX), vmem(8, BOX), vmem(2, deep, BOX), vmem(2, deep, BOX),
             vmem(8, BOX), vmem(8, BOX), vmem(2, BOX, BOX), vmem(2, 8, BOX),
@@ -564,8 +531,8 @@
             vmem(bands, 2, ext2, ext1, dtype=BF16), vmem(bands, 2, BOX, ext2, dtype=BF16),
             vmem(2, 2, NAR, NAR, dtype=BF16), vmem(2, NAR, NAR, dtype=BF16),
             vmem(ext1, NAR, dtype=BF16), vmem(ext1, NAR, dtype=BF16),
-            pltpu.SemaphoreType.DMA((9,)), pltpu.SemaphoreType.DMA((5,)),
-            pltpu.SemaphoreType.DMA((5,)), pltpu.SemaphoreType.DMA((2, 4)),
+            pltpu.SemaphoreType.DMA((9,)), pltpu.SemaphoreType.DMA((6,)),
+            pltpu.SemaphoreType.DMA((6,)), pltpu.SemaphoreType.DMA((2, 4)),
             pltpu.SemaphoreType.DMA((2, 10)), pltpu.SemaphoreType.DMA((2, 2)),
         ]
         anywhere = pl.BlockSpec(memory_space=pl.ANY)
@@ -573,23 +540,26 @@
         shapes = tuple(
             jax.ShapeDtypeStruct(a.shape, F32) for a in (observed, morph, sed)
         )
+        operands = (
+            observed, inverse_variance, sed, morph, foot_block, gamma, row_kernel, col_kernel
+        )
         results = pl.pallas_call(
             functools.partial(kernel, nty, ntx, bands, taps),
             out_shape=shapes,
             in_specs=[pl.BlockSpec(memory_space=pltpu.HBM)] * 8,
-            out_specs=(anywhere, vector, vector),
+            out_specs=(vector, vector, vector),
             scratch_shapes=scratch,
-            compiler_params=pltpu.CompilerParams(collective_id=0, has_side_effects=True),
-        )(observed, inverse_variance, sed, morph, foot_block, gamma, row_kernel, col_kernel)
+            compiler_params=pltpu.CompilerParams(
+                collective_id=0, has_side_effects=True, vmem_limit_bytes=40 * 2**20
+            ),
+        )(*(a if a.size == 1 else pltpu.with_memory_space_constraint(a, pltpu.HBM) for a in operands))
         return pl.pallas_call(
             write_out,
             out_shape=shapes,
-            in_specs=[anywhere] * 3,
+            in_specs=[vector] * 3,
             out_specs=(anywhere,) * 3,
-            scratch_shapes=[
-                vmem(bands, height, width), vmem(*morph.shape), vmem(*sed.shape),
-                pltpu.SemaphoreType.DMA((bands + 2,)), pltpu.SemaphoreType.DMA((bands + 2,)),
-            ],
+            scratch_shapes=[pltpu.SemaphoreType.DMA((3,))],
+            compiler_params=pltpu.CompilerParams(vmem_limit_bytes=8 * 2**20),
         )(*results)
 
     in_specs = (

time: 65.9 us -> 60.1 us (0.912)
  Pallas kernels: 63.8 us -> 58.1 us
    pallas_call x1, Pallas kernels: 61.8 us -> 57.1 us  [body(): pl.pallas_call(functools.partial(kernel, nty, ntx, bands, taps), out_shap...]
    pallas_call x1, Pallas kernels: 2.02 us -> 0.92 us  [body(): pl.pallas_call(write_out, out_shape=shapes, in_specs=[vector] * 3, out_sp...]
where the time goes in v3:
time: 60.1 us; the launch traced here: 60 us
  Pallas kernels  58.1 us (97%)
  between operations  1.93 us (3%)
    pallas_call x1, Pallas kernels, body(): pl.pallas_call(functools.partial(kernel, nty, ntx, bands, taps), out_shap...  57.1 us

profile of v3, /device:TPU:1, one launch (start us, length us, event | category | flops | bytes accessed | tf_op | source)
XLA Modules:
  0.0 60.0 jit_solution(8892379733780956702)
XLA Ops:
  1.9 57.1 %shard_map.103 = (f32[6,128,256]{2,1,0:T(8,128)S(1)}, f32[1,1,128,128]{3,2,1,0:T(8,128)S(1)}, f32[1,1,6]{2,1,0:T(1,128)S(1)}) custom-call(f32[6,128,256]{2,1,0:T(8,128)} %obs_hbm.1, f32[6,128,256]{2,1,0:T(8,128)} %iv_hbm.1, f32[1,1,6]{2,1,0:T(1,128)} %sed_hbm.1, f32[1,1,128,128]{3,2,1,0:T(8,128)} %morph_hbm.1, s32[1,1]{1,0:T(1,128)S(6)} %copy.11.foot_hbm, ...), custom_call_target="tpu_custom_call" | custom-call | tf_op jit(solution)/shard_map/pallas_call | solution.py:546
  59.1 0.9 %shard_map.104 = (f32[6,128,256]{2,1,0:T(8,128)}, f32[1,1,128,128]{3,2,1,0:T(8,128)}, f32[1,1,6]{2,1,0:T(1,128)}) custom-call(f32[6,128,256]{2,1,0:T(8,128)S(1)} %get-tuple-element.6.resid, f32[1,1,128,128]{3,2,1,0:T(8,128)S(1)} %get-tuple-element.7.morph, f32[1,1,6]{2,1,0:T(1,128)S(1)} %get-tuple-element.8.sed), custom_call_target="tpu_custom_call" | custom-call | tf_op jit(solution)/shard_map/pallas_call | solution.py:556

commit v4 on v3

--- a/solution.py
+++ b/solution.py
@@ -32,6 +32,15 @@
 
 def exact(a, b):
     return jnp.dot(a, b, preferred_element_type=F32, precision=HIGHEST)
+
+
+def gather(pick, x):
+    hi = x.astype(BF16)
+    rest = x - hi.astype(F32)
+    mid = rest.astype(BF16)
+    low = (rest - mid.astype(F32)).astype(BF16)
+    pick = pick.astype(BF16)
+    return (dot(pick, hi) + dot(pick, mid)) + dot(pick, low)
 
 
 def kernel(
@@ -198,7 +207,6 @@
     strip_tables(0)
 
     whole(info_in, 5).wait_recv()
-    whole(ib1, 0).wait_recv()
     infos = info_in[:, 0, :]
     wide = (ntx, BOX)
     row_i, lane_i = iota(wide, 0), iota(wide, 1)
@@ -215,8 +223,9 @@
         jnp.where((tile_row == target) & (slot_row == float(s)), 1.0, 0.0)[:, 0:ntx]
         for s in range(2)
     ]
+    whole(ib1, 0).wait_recv()
     pieces = jnp.concatenate([ib1[:, r, :] for r in range(rows)], axis=1)
-    chosen = exact(jnp.concatenate(pick, axis=0), pieces)
+    chosen = gather(jnp.concatenate(pick, axis=0), pieces)
     for s in range(2):
         for r in range(rows):
             ob2[:, s * rows + r, :] = chosen[
@@ -307,9 +316,8 @@
 
     def along_rows(trow, b, image):
         hi, lo = split(image)
-        count, depth = trow.shape[2:]
-        both = dot(trow[b].reshape(2 * count, depth), hi)
-        return both[:count] + (both[count:] + dot(trow[b, 0], lo))
+        both = dot(trow[b, 0], jnp.concatenate([hi, lo], axis=1))
+        return both[:, 0:BOX] + (both[:, BOX:] + dot(trow[b, 1], hi))
 
     for b in range(bands):
         mixed_e[b, deep : deep + BOX] = columns(0, b, model_e[b, deep : deep + BOX])
@@ -341,6 +349,30 @@
     load_iv.wait()
     for copy in images:
         copy.wait_recv()
+
+    half = BOX // 2
+    row, lane = iota((ext2, BOX), 0), iota((ext2, BOX), 1)
+    inside = ((row >= HALO) | (ti > 0)) & ((row < HALO + BOX) | (ti < nty - 1))
+    near = iota((ext1, BOX), 1) < half
+
+    def residual_of(b, mixed, flipped):
+        predicted = along_rows(trow1, b, mixed)
+        first = (lane < half) != flipped
+        seen = jnp.where(first, obs_e[b, :, 0:BOX], obs_e[b, :, BOX:])
+        weights = jnp.where(first, iv_e[b, :, 0:BOX], iv_e[b, :, BOX:])
+        residual = jnp.where(inside, weights * (seen - predicted), 0.0)
+        image = along_rows(trow2, b, residual)
+        middle = residual[HALO : HALO + BOX]
+        low = slice(BOX, BOX + half) if flipped else slice(0, half)
+        high = slice(half, BOX) if flipped else slice(BOX + half, 2 * BOX)
+        for ref, values in ((resid_ref, middle), (back, image)):
+            ref[b, :, low] = values[:, 0:half]
+            ref[b, :, high] = values[:, half:]
+        return image
+
+    for b in range(bands):
+        residual_of(b, jnp.where(near, mixed_e[b, :, BOX:], mixed_e[b, :, 0:BOX]), True)
+
     for copy in waits[4:]:
         copy.wait_recv()
 
@@ -354,26 +386,18 @@
 
     halo_parts(west1, east1, ext1, deep)
     pack[...] = three(ext_h[...], ext_l[...], diag[0, 0], diag[0, 1])
-    row = iota((ext2, 2 * BOX), 0)
-    inside = ((row >= HALO) | (ti > 0)) & ((row < HALO + BOX) | (ti < nty - 1))
     first_lanes = iota((ext1, BOX), 1) < reach
     last_lanes = iota((ext1, BOX), 1) >= BOX - reach
-
     to_west = to_east = jnp.zeros((BOX, BOX), F32)
     for b in range(bands):
         left = pltpu.roll(pack[:, 0:BOX], (BOX - reach * b) % BOX, 1)
-        left = mixed_e[b, :, 0:BOX] + jnp.where(first_lanes, left, 0.0)
         right = pltpu.roll(pack[:, BOX:], (2 * BOX - reach - reach * b) % BOX, 1)
-        right = mixed_e[b, :, BOX:] + jnp.where(last_lanes, right, 0.0)
-        predicted = along_rows(trow1, b, jnp.concatenate([left, right], axis=1))
-        residual = jnp.where(inside, iv_e[b] * (obs_e[b] - predicted), 0.0)
-        resid_ref[b] = residual[HALO : HALO + BOX]
-        image = along_rows(trow2, b, residual)
-        back[b] = image
+        mixed = jnp.where(near, mixed_e[b, :, 0:BOX], mixed_e[b, :, BOX:])
+        mixed = mixed + jnp.where(first_lanes, left, jnp.where(last_lanes, right, 0.0))
+        image = residual_of(b, mixed, False)
         keep = of_band(tile_lane, b)
-        to_west = jnp.where(keep, pltpu.roll(image[:, 0:BOX], reach * b, 1), to_west)
-        moved = pltpu.roll(image[:, BOX:], (reach * b + reach) % BOX, 1)
-        to_east = jnp.where(keep, moved, to_east)
+        to_west = jnp.where(keep, pltpu.roll(image, reach * b, 1), to_west)
+        to_east = jnp.where(keep, pltpu.roll(image, (reach * b + reach) % BOX, 1), to_east)
     sw2[...] = to_west
     se2[...] = to_east
     strips = [
@@ -456,7 +480,7 @@
         ],
         axis=0,
     )
-    chosen = exact(give, pieces)
+    chosen = gather(give, pieces)
     for r in range(rows):
         ob4[:, r, :] = chosen[:, r * BOX : (r + 1) * BOX]
     exchange(ob4, ib4, 3)

time: 60.1 us -> 60.4 us (level)
  no operation moved by 1% of the time
where the time goes in v4:
time: 60.4 us; the launch traced here: 60.3 us
  Pallas kernels  58.4 us (97%)
  between operations  1.93 us (3%)
    pallas_call x1, Pallas kernels, body(): pl.pallas_call(functools.partial(kernel, nty, ntx, bands, taps), out_shap...  57.4 us

profile of v4, /device:TPU:1, one launch (start us, length us, event | category | flops | bytes accessed | tf_op | source)
XLA Modules:
  0.0 60.3 jit_solution(15711883761904176785)
XLA Ops:
  1.9 57.4 %shard_map.103 = (f32[6,128,256]{2,1,0:T(8,128)S(1)}, f32[1,1,128,128]{3,2,1,0:T(8,128)S(1)}, f32[1,1,6]{2,1,0:T(1,128)S(1)}) custom-call(f32[6,128,256]{2,1,0:T(8,128)} %obs_hbm.1, f32[6,128,256]{2,1,0:T(8,128)} %iv_hbm.1, f32[1,1,6]{2,1,0:T(1,128)} %sed_hbm.1, f32[1,1,128,128]{3,2,1,0:T(8,128)} %morph_hbm.1, s32[1,1]{1,0:T(1,128)S(6)} %copy.11.foot_hbm, ...), custom_call_target="tpu_custom_call" | custom-call | tf_op jit(solution)/shard_map/pallas_call | solution.py:570
  59.4 0.9 %shard_map.104 = (f32[6,128,256]{2,1,0:T(8,128)}, f32[1,1,128,128]{3,2,1,0:T(8,128)}, f32[1,1,6]{2,1,0:T(1,128)}) custom-call(f32[6,128,256]{2,1,0:T(8,128)S(1)} %get-tuple-element.6.resid, f32[1,1,128,128]{3,2,1,0:T(8,128)S(1)} %get-tuple-element.7.morph, f32[1,1,6]{2,1,0:T(1,128)S(1)} %get-tuple-element.8.sed), custom_call_target="tpu_custom_call" | custom-call | tf_op jit(solution)/shard_map/pallas_call | solution.py:580

commit v5 on v3

--- a/solution.py
+++ b/solution.py
@@ -32,6 +32,15 @@
 
 def exact(a, b):
     return jnp.dot(a, b, preferred_element_type=F32, precision=HIGHEST)
+
+
+def gather(pick, x):
+    hi = x.astype(BF16)
+    rest = x - hi.astype(F32)
+    mid = rest.astype(BF16)
+    low = (rest - mid.astype(F32)).astype(BF16)
+    pick = pick.astype(BF16)
+    return (dot(pick, hi) + dot(pick, mid)) + dot(pick, low)
 
 
 def kernel(
@@ -198,7 +207,6 @@
     strip_tables(0)
 
     whole(info_in, 5).wait_recv()
-    whole(ib1, 0).wait_recv()
     infos = info_in[:, 0, :]
     wide = (ntx, BOX)
     row_i, lane_i = iota(wide, 0), iota(wide, 1)
@@ -215,8 +223,9 @@
         jnp.where((tile_row == target) & (slot_row == float(s)), 1.0, 0.0)[:, 0:ntx]
         for s in range(2)
     ]
+    whole(ib1, 0).wait_recv()
     pieces = jnp.concatenate([ib1[:, r, :] for r in range(rows)], axis=1)
-    chosen = exact(jnp.concatenate(pick, axis=0), pieces)
+    chosen = gather(jnp.concatenate(pick, axis=0), pieces)
     for s in range(2):
         for r in range(rows):
             ob2[:, s * rows + r, :] = chosen[
@@ -288,12 +297,12 @@
             ref[...] = jnp.where(keep, moved, ref[...])
     for n, (src, dst, yy, xx) in enumerate(
         (
-            (se1, west1.at[deep : deep + BOX], ti, east),
-            (sw1, east1.at[deep : deep + BOX], ti, west),
             (se1.at[BOX - deep : BOX], west1.at[0:deep], south, east),
             (sw1.at[BOX - deep : BOX], east1.at[0:deep], south, west),
             (se1.at[0:deep], west1.at[deep + BOX : ext1], north, east),
             (sw1.at[0:deep], east1.at[deep + BOX : ext1], north, west),
+            (se1, west1.at[deep : deep + BOX], ti, east),
+            (sw1, east1.at[deep : deep + BOX], ti, west),
         )
     ):
         waits.append(send(src, dst, sl_sem.at[0, 4 + n], sl_sem.at[1, 4 + n], yy, xx))
@@ -456,7 +465,7 @@
         ],
         axis=0,
     )
-    chosen = exact(give, pieces)
+    chosen = gather(give, pieces)
     for r in range(rows):
         ob4[:, r, :] = chosen[:, r * BOX : (r + 1) * BOX]
     exchange(ob4, ib4, 3)

time: 60.1 us -> 59.8 us (level)
  no operation moved by 1% of the time
where the time goes in v5:
time: 59.8 us; the launch traced here: 59.6 us
  Pallas kernels  57.7 us (96%)
  between operations  1.93 us (3%)
    pallas_call x1, Pallas kernels, body(): pl.pallas_call(functools.partial(kernel, nty, ntx, bands, taps), out_shap...  56.8 us

profile of v5, /device:TPU:1, one launch (start us, length us, event | category | flops | bytes accessed | tf_op | source)
XLA Modules:
  0.0 59.6 jit_solution(12545098925994888497)
XLA Ops:
  1.9 56.8 %shard_map.103 = (f32[6,128,256]{2,1,0:T(8,128)S(1)}, f32[1,1,128,128]{3,2,1,0:T(8,128)S(1)}, f32[1,1,6]{2,1,0:T(1,128)S(1)}) custom-call(f32[6,128,256]{2,1,0:T(8,128)} %obs_hbm.1, f32[6,128,256]{2,1,0:T(8,128)} %iv_hbm.1, f32[1,1,6]{2,1,0:T(1,128)} %sed_hbm.1, f32[1,1,128,128]{3,2,1,0:T(8,128)} %morph_hbm.1, s32[1,1]{1,0:T(1,128)S(6)} %copy.11.foot_hbm, ...), custom_call_target="tpu_custom_call" | custom-call | tf_op jit(solution)/shard_map/pallas_call | solution.py:555
  58.7 0.9 %shard_map.104 = (f32[6,128,256]{2,1,0:T(8,128)}, f32[1,1,128,128]{3,2,1,0:T(8,128)}, f32[1,1,6]{2,1,0:T(1,128)}) custom-call(f32[6,128,256]{2,1,0:T(8,128)S(1)} %get-tuple-element.6.resid, f32[1,1,128,128]{3,2,1,0:T(8,128)S(1)} %get-tuple-element.7.morph, f32[1,1,6]{2,1,0:T(1,128)S(1)} %get-tuple-element.8.sed), custom_call_target="tpu_custom_call" | custom-call | tf_op jit(solution)/shard_map/pallas_call | solution.py:565

commit v6 on v5

--- a/solution.py
+++ b/solution.py
@@ -71,11 +71,10 @@
         return jnp.where(p >= ntx, p - ntx, p)
 
     order = sorted(range(1, ntx), key=lambda j: -min(j, ntx - j))
-    for j in order:
-        pl.semaphore_signal(barrier, inc=1, device_id=(ti, wrapped(j)), device_id_type=MESH)
-    for yy in (north, south):
-        for xx in (me, west, east):
-            pl.semaphore_signal(barrier, inc=1, device_id=(yy, xx), device_id_type=MESH)
+    greeted = [(ti, wrapped(j)) for j in order]
+    beyond = [(yy, xx) for xx in (west, east, me) for yy in (north, south)]
+    for yy, xx in greeted[:12] + beyond + greeted[12:]:
+        pl.semaphore_signal(barrier, inc=1, device_id=(yy, xx), device_id_type=MESH)
 
     load_morph = pltpu.make_async_copy(morph_hbm.at[0, 0], morph_v, loc_sem.at[0])
     load_rk = pltpu.make_async_copy(rk_hbm, rk_v, loc_sem.at[1])

time: 59.8 us -> 59.6 us (level)
  no operation moved by 1% of the time
where the time goes in v6:
time: 59.6 us; the launch traced here: 59.4 us
  Pallas kernels  57.5 us (96%)
  between operations  1.93 us (3%)
    pallas_call x1, Pallas kernels, body(): pl.pallas_call(functools.partial(kernel, nty, ntx, bands, taps), out_shap...  56.6 us

profile of v6, /device:TPU:1, one launch (start us, length us, event | category | flops | bytes accessed | tf_op | source)
XLA Modules:
  0.0 59.4 jit_solution(5762259329750132832)
XLA Ops:
  1.9 56.6 %shard_map.103 = (f32[6,128,256]{2,1,0:T(8,128)S(1)}, f32[1,1,128,128]{3,2,1,0:T(8,128)S(1)}, f32[1,1,6]{2,1,0:T(1,128)S(1)}) custom-call(f32[6,128,256]{2,1,0:T(8,128)} %obs_hbm.1, f32[6,128,256]{2,1,0:T(8,128)} %iv_hbm.1, f32[1,1,6]{2,1,0:T(1,128)} %sed_hbm.1, f32[1,1,128,128]{3,2,1,0:T(8,128)} %morph_hbm.1, s32[1,1]{1,0:T(1,128)S(6)} %copy.11.foot_hbm, ...), custom_call_target="tpu_custom_call" | custom-call | tf_op jit(solution)/shard_map/pallas_call | solution.py:554
  58.5 0.9 %shard_map.104 = (f32[6,128,256]{2,1,0:T(8,128)}, f32[1,1,128,128]{3,2,1,0:T(8,128)}, f32[1,1,6]{2,1,0:T(1,128)}) custom-call(f32[6,128,256]{2,1,0:T(8,128)S(1)} %get-tuple-element.6.resid, f32[1,1,128,128]{3,2,1,0:T(8,128)S(1)} %get-tuple-element.7.morph, f32[1,1,6]{2,1,0:T(1,128)S(1)} %get-tuple-element.8.sed), custom_call_target="tpu_custom_call" | custom-call | tf_op jit(solution)/shard_map/pallas_call | solution.py:564

commit v7 on v6

--- a/solution.py
+++ b/solution.py
@@ -237,6 +237,10 @@
         mine = (tile_col == here) & (slot_col == float(s))
         sinfo[pl.ds(s, 1), :] = jnp.sum(jnp.where(mine, infos, 0.0), axis=0, keepdims=True)
     sinfo[2:8, :] = jnp.zeros((6, BOX), F32)
+    heads = [
+        send(sinfo, ninfo, sl_sem.at[0, 2], sl_sem.at[1, 2], south, me),
+        send(sinfo, soinfo, sl_sem.at[0, 3], sl_sem.at[1, 3], north, me),
+    ]
     lane_f = lane_i.astype(F32)
     give = jnp.concatenate(
         [
@@ -277,8 +281,6 @@
         (
             (slots.at[:, BOX - deep : BOX, :], nslots, south),
             (slots.at[:, 0:deep, :], sslots, north),
-            (sinfo, ninfo, south),
-            (sinfo, soinfo, north),
         )
     ):
         waits.append(send(src, dst, sl_sem.at[0, n], sl_sem.at[1, n], yy, me))
@@ -322,10 +324,12 @@
     for b in range(bands):
         mixed_e[b, deep : deep + BOX] = columns(0, b, model_e[b, deep : deep + BOX])
 
-    for copy in waits[0:4]:
+    for copy in heads:
         copy.wait_recv()
     tables(0, ninfo, jnp.where(ti > 0, 1.0, 0.0))
     tables(2, soinfo, jnp.where(ti < nty - 1, 1.0, 0.0))
+    for copy in waits[0:2]:
+        copy.wait_recv()
 
     for b in range(bands):
         image = jnp.concatenate(
@@ -349,7 +353,7 @@
     load_iv.wait()
     for copy in images:
         copy.wait_recv()
-    for copy in waits[4:]:
+    for copy in waits[2:]:
         copy.wait_recv()
 
     def halo_parts(left, right, count, edge):
@@ -490,7 +494,7 @@
 
     for phase, arrived in enumerate((ib1, ib2, ib3, ib4, sg_in, info_in)):
         whole(arrived, phase).wait_send()
-    for copy in images + waits + strips:
+    for copy in images + heads + waits + strips:
         copy.wait_send()
 
 

time: 59.6 us -> 59.6 us (level)
  no operation moved by 1% of the time
where the time goes in v7:
time: 59.6 us; the launch traced here: 59.5 us
  Pallas kernels  57.5 us (96%)
  between operations  1.93 us (3%)
    pallas_call x1, Pallas kernels, body(): pl.pallas_call(functools.partial(kernel, nty, ntx, bands, taps), out_shap...  56.6 us

profile of v7, /device:TPU:1, one launch (start us, length us, event | category | flops | bytes accessed | tf_op | source)
XLA Modules:
  0.0 59.5 jit_solution(7723048909054749914)
XLA Ops:
  1.9 56.6 %shard_map.103 = (f32[6,128,256]{2,1,0:T(8,128)S(1)}, f32[1,1,128,128]{3,2,1,0:T(8,128)S(1)}, f32[1,1,6]{2,1,0:T(1,128)S(1)}) custom-call(f32[6,128,256]{2,1,0:T(8,128)} %obs_hbm.1, f32[6,128,256]{2,1,0:T(8,128)} %iv_hbm.1, f32[1,1,6]{2,1,0:T(1,128)} %sed_hbm.1, f32[1,1,128,128]{3,2,1,0:T(8,128)} %morph_hbm.1, s32[1,1]{1,0:T(1,128)S(6)} %copy.11.foot_hbm, ...), custom_call_target="tpu_custom_call" | custom-call | tf_op jit(solution)/shard_map/pallas_call | solution.py:558
  58.6 0.9 %shard_map.104 = (f32[6,128,256]{2,1,0:T(8,128)}, f32[1,1,128,128]{3,2,1,0:T(8,128)}, f32[1,1,6]{2,1,0:T(1,128)}) custom-call(f32[6,128,256]{2,1,0:T(8,128)S(1)} %get-tuple-element.6.resid, f32[1,1,128,128]{3,2,1,0:T(8,128)S(1)} %get-tuple-element.7.morph, f32[1,1,6]{2,1,0:T(1,128)S(1)} %get-tuple-element.8.sed), custom_call_target="tpu_custom_call" | custom-call | tf_op jit(solution)/shard_map/pallas_call | solution.py:568
